TPU v7x, 256 devices: a whole 4x4x8 slice. The times are simulated.
256 devices in a mesh: ctx: 32 (over y, z_lo, core), tp: 8 (over x, z_hi).
Axes of the slice: x: 4, y: 4, z: 8 (z_hi: 2, z_lo: 4; z = z_hi * 4 + z_lo), core: 2. Of those that a mesh axis runs over, the one named last changes fastest.
Arguments:
- tokens: bfloat16 [12288, 3072], P('ctx', 'tp'), may hold values from -6 to 6
- queries: bfloat16 [12288, 2048], P('ctx', 'tp'), may hold values from -16 to 16
- key_rows: bfloat16 [12288, 2048], P('ctx', 'tp'), may hold values from -16 to 16
- value_rows: bfloat16 [12288, 2048], P('ctx', 'tp'), may hold values from -6 to 6
- clip_ids: int32 [12288], replicated, may hold values from 0 to 3, never falling along the last dimension, each value on 1 to 9216 neighbouring positions
- causal: int32 [4], replicated, may hold values 0 or 1
- modulation: float32 [3, 4, 3072], replicated, may hold values from -3 to 3
- w_mlp: bfloat16 [3072, 6144], P(None, 'tp'), may hold values from -0.109375 to 0.109375
- w_attn_out: bfloat16 [2048, 3072], P('tp'), may hold values from -1 to 1
- w_mlp_out: bfloat16 [6144, 3072], P('tp'), may hold values from -0.078125 to 0.078125
Outputs:
- mixed: float32 [12288, 3072], P(('ctx', 'tp'))
Inputs may be any that keep to these rules, and one draw needn't show every extreme that they name: `clip_ids`: clip numbers never fall along the tokens; each of the 4 clips has 1 to 9216 tokens and one has exactly 9216.
All inputs are finite; a program needn't handle non-finite values.
Results may differ from a plain program's by a relative error of at most 0.0065.
Values may be sent and summed in bfloat16 or wider, within the bound.
A program may use at most 128 MiB of HBM per device.

v0:
```python
import math

import jax
import jax.numpy as jnp
from jax import lax
from jax.sharding import PartitionSpec as P

HD = 128


neg_large = -1e30
eps_norm = 1e-06


def per_token(clip_rows, table):
    onehot = (clip_rows[:, None] == jnp.arange(table.shape[0], dtype=jnp.int32)[None, :]).astype(
        jnp.float32
    )
    return jnp.dot(onehot, table, precision=lax.Precision.HIGHEST)


def causal_rows(clip_rows, causal):
    matches = clip_rows[:, None] == jnp.arange(causal.shape[0], dtype=jnp.int32)[None, :]
    return jnp.sum(jnp.where(matches, causal[None, :], 0), axis=1)


def visible(query_ids, query_pos, query_causal, key_ids, key_pos):
    same_clip = query_ids[:, None] == key_ids[None, :]
    earlier = key_pos[None, :] <= query_pos[:, None]
    return same_clip & ((query_causal[:, None] == 0) | earlier)


def attend(carry_state, query_tile, allowed, key_tile, value_tile, inverse_root):
    numerator, running_max, denominator = carry_state
    scores = (
        jnp.einsum("ihd,jhd->hij", query_tile, key_tile, preferred_element_type=jnp.float32)
        * inverse_root
    )
    scores = jnp.where(allowed[None], scores, neg_large)
    new_max = jnp.maximum(running_max, jnp.transpose(jnp.max(scores, axis=2)))
    weights = jnp.where(allowed[None], jnp.exp(scores - jnp.transpose(new_max)[:, :, None]), 0.0)
    rounded = weights.astype(jnp.bfloat16)
    factor = jnp.exp(running_max - new_max)
    numerator = numerator * factor[:, :, None] + jnp.einsum(
        "hij,jhd->ihd", rounded, value_tile, preferred_element_type=jnp.float32
    )
    denominator = denominator * factor + jnp.transpose(jnp.sum(rounded.astype(jnp.float32), axis=2))
    return (numerator, new_max, denominator)


def attend_some(carry_state, query_tile, allowed, key_tile, value_tile, inverse_root):
    return attend(carry_state, query_tile, allowed, key_tile, value_tile, inverse_root)


def per_device(
    tokens,
    queries,
    key_rows,
    value_rows,
    clip_ids,
    causal,
    modulation,
    w_mlp,
    w_attn_out,
    w_mlp_out,
):
    local_rows = queries.shape[0]
    heads_local = queries.shape[1] // HD
    inverse_root = 1.0 / math.sqrt(HD)
    tp_size = lax.axis_size("tp")
    first_row = lax.axis_index("ctx") * local_rows
    own_pos = first_row + jnp.arange(local_rows, dtype=jnp.int32)
    own_ids = lax.dynamic_slice_in_dim(clip_ids, first_row, local_rows)
    own_causal = causal_rows(own_ids, causal)
    own_query = queries.reshape(local_rows, heads_local, HD)
    start_state = (
        jnp.zeros((local_rows, heads_local, HD), jnp.float32),
        jnp.full((local_rows, heads_local), neg_large, jnp.float32),
        jnp.zeros((local_rows, heads_local), jnp.float32),
    )
    whole_rows = lax.all_gather(tokens, "tp", axis=1, tiled=True)
    token_values = whole_rows.astype(jnp.float32)
    row_mean = jnp.mean(token_values, axis=1, keepdims=True)
    centred = token_values - row_mean
    row_var = jnp.mean(centred * centred, axis=1, keepdims=True)
    normed = centred * lax.rsqrt(row_var + eps_norm)
    shift_rows = per_token(own_ids, modulation[0])
    scale_rows = per_token(own_ids, modulation[1])
    modulated = (normed * (1.0 + scale_rows) + shift_rows).astype(jnp.bfloat16)
    hidden = jax.nn.gelu(
        jnp.dot(modulated, w_mlp, preferred_element_type=jnp.float32), approximate=True
    ).astype(jnp.bfloat16)
    carry_state = start_state
    key_piece = lax.all_gather(key_rows, "ctx", axis=0, tiled=True)
    value_piece = lax.all_gather(value_rows, "ctx", axis=0, tiled=True)
    piece_rows = key_piece.shape[0]
    tile_rows = piece_rows
    tile_rows = local_rows * math.gcd(piece_rows // local_rows, 4)

    def one_tile(inner_state, tile_index):
        offset = tile_index * tile_rows
        key_tile = lax.dynamic_slice_in_dim(key_piece, offset, tile_rows, 0).reshape(
            tile_rows, heads_local, HD
        )
        value_tile = lax.dynamic_slice_in_dim(value_piece, offset, tile_rows, 0).reshape(
            tile_rows, heads_local, HD
        )
        key_pos = offset + jnp.arange(tile_rows, dtype=jnp.int32)
        key_ids = lax.dynamic_slice_in_dim(clip_ids, offset, tile_rows)
        allowed = visible(own_ids, own_pos, own_causal, key_ids, key_pos)
        return (
            attend_some(inner_state, own_query, allowed, key_tile, value_tile, inverse_root),
            None,
        )

    carry_state, _ = lax.scan(
        one_tile, carry_state, jnp.arange(piece_rows // tile_rows, dtype=jnp.int32)
    )
    numerator, running_max, denominator = carry_state
    attended = (
        (numerator / denominator[:, :, None])
        .astype(jnp.bfloat16)
        .reshape(local_rows, heads_local * HD)
    )
    share_rows = local_rows // tp_size
    branch = lax.psum_scatter(
        jnp.dot(attended, w_attn_out, preferred_element_type=jnp.float32)
        + jnp.dot(hidden, w_mlp_out, preferred_element_type=jnp.float32),
        "tp",
        scatter_dimension=0,
        tiled=True,
    )
    first_share = lax.axis_index("tp") * share_rows
    residual = lax.dynamic_slice_in_dim(token_values, first_share, share_rows, 0)
    gate_rows = lax.dynamic_slice_in_dim(
        per_token(own_ids, modulation[2]), first_share, share_rows, 0
    )
    return residual + gate_rows * branch


def solution(mesh):
    in_specs = (
        P("ctx", "tp"),
        P("ctx", "tp"),
        P("ctx", "tp"),
        P("ctx", "tp"),
        P(),
        P(),
        P(),
        P(None, "tp"),
        P("tp", None),
        P("tp", None),
    )
    out_specs = P(("ctx", "tp"), None)
    return jax.shard_map(
        per_device, mesh=mesh, in_specs=in_specs, out_specs=out_specs, check_vma=False
    )
```

profile of v0, /device:TPU:112, one launch (start us, length us, event | category | flops | bytes accessed | tf_op | source)
XLA Modules:
  0.0 490.5 jit_solution(2514441145359709445)
XLA Ops:
  14.3 5.0 %fusion.19 = f32[384,3072]{1,0:T(8,128)} fusion(f32[3,4,3072]{2,1,0:T(4,128)} %param.18, s32[384]{0:T(512)S(1)} %dynamic_slice.23), kind=kOutput, calls=%fused_computation.40 | convolution fusion | flops 56624640 | bytes 4769280 | tf_op jit(solution)/shard_map/dot_general | solution.py:19
  19.3 68.5 %all-gather.4.cloned.1.call-done = bf16[384,3072]{1,0:T(8,128)(2,1)} async-done(((bf16[384,384]{1,0:T(8,128)(2,1)}), bf16[384,3072]{1,0:T(8,128)(2,1)}) %all-gather.4.cloned.1.call-update) | async-done | bytes 2359312 | tf_op jit(solution)/shard_map/all_gather | solution.py:81
  92.5 6.9 %add_convert_fusion = bf16[384,3072]{1,0:T(8,128)(2,1)} fusion(f32[384,3072]{1,0:T(8,128)} %fusion.19, bf16[384,3072]{1,0:T(8,128)(2,1)S(1)} %copy-done.2, f32[384]{0:T(512)S(1)} %add_rsqrt_fusion, f32[384]{0:T(512)S(1)} %broadcast_multiply_fusion, f32[3,4,3072]{2,1,0:T(4,128)} %param.18, s32[384]{0:T(512)S(1)} %dynamic_slice.23), kind=kOutput, calls=%fused_computation.19 | convolution fusion | flops 64882176 | bytes 9490944 | tf_op jit(solution)/shard_map/dot_general | solution.py:19
  99.4 11.6 %fusion.12 = f32[384,3072]{1,0:T(8,128)} fusion(bf16[768,3072]{1,0:T(8,128)(2,1)} %param.21, bf16[384,3072]{1,0:T(8,128)(2,1)} %add_convert_fusion, bf16[3072,768]{1,0:T(8,128)(2,1)} %param.19), kind=kOutput, calls=%fused_computation.32 | convolution fusion | flops 3626532864 | bytes 16515072 | tf_op jit(solution)/shard_map/dot_general | solution.py:128
  111.0 43.8 %all-gather.6.cloned.1.call-done = bf16[12288,256]{0,1:T(8,128)(2,1)} async-done(((bf16[384,256]{0,1:T(8,128)(2,1)}), bf16[12288,256]{0,1:T(8,128)(2,1)}) %all-gather.6.cloned.1.call-update) | async-done | bytes 6291472 | tf_op jit(solution)/shard_map/all_gather | solution.py:94
  154.8 68.4 %all-gather.8.cloned.1.call-done = bf16[12288,256]{0,1:T(8,128)(2,1)} async-done(((bf16[384,256]{0,1:T(8,128)(2,1)}), bf16[12288,256]{0,1:T(8,128)(2,1)}) %all-gather.8.cloned.1.call-update) | async-done | bytes 6291472 | tf_op jit(solution)/shard_map/all_gather | solution.py:95
  223.6 118.4 %while.15 = (s32[]{:T(128)}, f32[384,2,128]{0,2,1:T(8,128)S(1)}, f32[384,2]{0,1:T(2,128)S(1)}, f32[384,2]{0,1:T(2,128)S(1)}, s32[384]{0:T(512)S(1)}, /*index=5*/...) while((s32[]{:T(128)}, f32[384,2,128]{0,2,1:T(8,128)S(1)}, ...), condition=%wide.region_4.5_spmd.clone, body=%wide.region_1.4_spmd.clone.sunk | while | flops 624334848 | bytes 41178116 | solution.py:116
  233.0 3.7 convert_reduce_fusion.3
  244.4 3.3 fusion.51
  247.8 3.7 convert_reduce_fusion.3
  259.2 3.3 fusion.51
  262.6 3.7 convert_reduce_fusion.3
  274.0 3.3 fusion.51
  277.4 3.7 convert_reduce_fusion.3
  288.8 3.3 fusion.51
  292.2 3.7 convert_reduce_fusion.3
  307.0 3.7 convert_reduce_fusion.3
  318.4 3.3 fusion.51
  321.8 3.7 convert_reduce_fusion.3
  333.2 3.3 fusion.51
  336.5 3.7 convert_reduce_fusion.3
  342.0 5.3 %convolution_add_fusion = f32[384,3072]{1,0:T(8,128)} fusion(f32[384,3072]{1,0:T(8,128)} %fusion.12, bf16[384,256]{0,1:T(8,128)(2,1)S(1)} %bitcast.71, bf16[256,3072]{1,0:T(8,128)(2,1)S(1)} %copy-done), kind=kOutput, calls=%fused_computation.21 | convolution fusion | flops 605159424 | bytes 11206656 | tf_op jit(solution)/shard_map/dot_general | solution.py:127
  347.3 5.1 %fusion.21 = f32[384,3072]{1,0:T(8,128)} fusion(f32[3,4,3072]{2,1,0:T(4,128)} %param.18, s32[384]{0:T(512)S(1)} %get-tuple-element.315), kind=kOutput, calls=%fused_computation.42 | convolution fusion | flops 56624640 | bytes 4769280 | tf_op jit(solution)/shard_map/dot_general | solution.py:19
  355.2 126.4 %reduce-scatter.2.cloned.1.call-done = f32[48,3072]{1,0:T(8,128)} async-done(((f32[384,3072]{1,0:T(8,128)}), f32[48,3072]{1,0:T(8,128)}) %reduce-scatter.2.cloned.1.call-update) | async-done | bytes 589840 | tf_op jit(solution)/shard_map/reduce_scatter | solution.py:126
  (137 shorter events, 81.0 us)
Async XLA Ops:
  6.5 335.5 %copy-start = (bf16[256,3072]{1,0:T(8,128)(2,1)S(1)}, bf16[256,3072]{1,0:T(8,128)(2,1)}, u32[]{:S(2)}) copy-start(bf16[256,3072]{1,0:T(8,128)(2,1)} %param.20) | copy-start | bytes 4718596
  6.5 81.3 %all-gather.4.cloned.1.call-start = ((), (), s32[]{:S(2)}) async-start(), calls=%async_computation.1 | async-start | bytes 2654208 | tf_op jit(solution)/shard_map/all_gather | solution.py:81
  7.3 147.5 %all-gather.6.cloned.1.call-start = ((), (), s32[]{:S(2)}) async-start(), calls=%async_computation.2 | async-start | bytes 6488064 | tf_op jit(solution)/shard_map/all_gather | solution.py:94
  9.1 214.0 %all-gather.8.cloned.1.call-start = ((), (), s32[]{:S(2)}) async-start(), calls=%async_computation.3 | async-start | bytes 6488064 | tf_op jit(solution)/shard_map/all_gather | solution.py:95
  10.9 470.7 %reduce-scatter.2.cloned.1.call-start = ((), (), s32[]{:S(2)}) async-start(), calls=%async_computation.4 | async-start | bytes 5308416 | tf_op jit(solution)/shard_map/reduce_scatter | solution.py:126
  87.8 4.6 copy-start.2
  233.0 3.8 copy-start.1
  247.8 3.8 copy-start.1
  262.5 3.8 copy-start.1
  277.3 3.8 copy-start.1
  292.2 3.8 copy-start.1
  307.0 3.8 copy-start.1
  321.7 3.8 copy-start.1
  336.5 3.8 copy-start.1
  347.3 5.1 %copy-start.3 = (bf16[384,3072]{1,0:T(8,128)(2,1)S(1)}, bf16[384,3072]{1,0:T(8,128)(2,1)}, u32[]{:S(2)}) copy-start(bf16[384,3072]{1,0:T(8,128)(2,1)} %all-gather.4.cloned.1.call-done) | copy-start | bytes 7077892
Sparse Core Ops, SparseCore 0:
  9.8 77.9 all-gather.3
  89.6 65.0 all-gather.5
  156.6 66.5 all-gather.7
  347.4 134.1 reduce-scatter.1
where the time goes:
time: 496 us; the launch traced here: 490 us
  waiting for transfers between devices  308 us (62%)
  matrix products  73.8 us (15%)
  other arithmetic  55.2 us (11%)
  local copies, waits for them, and re-layouts  34.7 us (7%)
  between operations  13.2 us (3%)
  loops' own time  5.58 us (1%)
    reduce_scatter x1, waiting for transfers between devices, per_device(): lax.psum_scatter(jnp.dot(attended, w_attn_out, preferred_element_type=jnp...  126 us
    all_gather x1, waiting for transfers between devices, per_device(): whole_rows = lax.all_gather(tokens, 'tp', axis=1, tiled=True)  68.5 us
    all_gather x1, waiting for transfers between devices, per_device(): value_piece = lax.all_gather(value_rows, 'ctx', axis=0, tiled=True)  68.4 us
    all_gather x1, waiting for transfers between devices, per_device(): key_piece = lax.all_gather(key_rows, 'ctx', axis=0, tiled=True)  43.8 us
    reduce_sum x8, other arithmetic, attend(): jnp.sum(rounded.astype(jnp.float32), axis=2)  29.8 us
    dot_general x8, matrix products, attend(): jnp.einsum('ihd,jhd->hij', query_tile, key_tile, preferred_element_type=j...  26.6 us
    dot_general x3, matrix products, per_token(): return jnp.dot(onehot, table, precision=lax.Precision.HIGHEST)  17 us
    dot_general x8, matrix products, attend(): jnp.einsum('hij,jhd->ihd', rounded, value_tile, preferred_element_type=jn...  13.4 us
  transfers between devices with their start and end apart: 4, of which 4 were waited for; matrix products, arithmetic and copies ran while one was open for 9% of the time, Pallas kernels for 0%

commit v1 on v0

v1 whole, which is shorter than its diff:
```python
import functools
import math

import jax
import jax.numpy as jnp
from jax import lax
from jax.experimental import pallas as pl
from jax.experimental.pallas import tpu as pltpu
from jax.sharding import PartitionSpec as P

HD = 128
TILE = 1024
neg_large = -1e30
eps_norm = 1e-06


def pick_rows(clip_rows, table):
    out = jnp.broadcast_to(table[0][None, :], (clip_rows.shape[0], table.shape[1]))
    for clip in range(1, table.shape[0]):
        out = jnp.where(clip_rows[:, None] == clip, table[clip][None, :], out)
    return out


def attend_kernel(bounds, q_ref, start_ref, end_ref, k_ref, v_ref, out_ref, acc, peak):
    step = pl.program_id(0)
    tile = bounds[0] + step
    factor = math.log2(math.e) / math.sqrt(HD)
    heads = q_ref.shape[1] // HD

    @pl.when(step == 0)
    def _():
        acc[...] = jnp.zeros_like(acc)
        peak[...] = jnp.full_like(peak, neg_large)

    def one_tile(masked):
        rows = q_ref.shape[0]
        if masked:
            pos = tile * TILE + lax.broadcasted_iota(jnp.int32, (rows, TILE), 1)
            allowed = (pos >= start_ref[...]) & (pos < end_ref[...])
        ones = jnp.ones((TILE, HD), jnp.bfloat16)
        for head in range(heads):
            cols = slice(head * HD, (head + 1) * HD)
            scores = lax.dot_general(
                q_ref[:, cols], k_ref[:, cols], (((1,), (1,)), ((), ())),
                preferred_element_type=jnp.float32,
            )
            if masked:
                scores = jnp.where(allowed, scores, neg_large)
            old = peak[head]
            new = jnp.maximum(old, jnp.max(scores, axis=1, keepdims=True))
            weights = jnp.exp2((scores - new[:, :1]) * factor)
            if masked:
                weights = jnp.where(allowed, weights, 0.0)
            shrink = jnp.exp2((old - new) * factor)
            values = jnp.concatenate([v_ref[:, cols], ones], axis=1)
            added = jnp.dot(
                weights.astype(jnp.bfloat16), values, preferred_element_type=jnp.float32
            )
            acc[head] = acc[head] * jnp.concatenate([shrink, shrink], axis=1) + added
            peak[head] = new

    active = tile < bounds[1]
    whole = (tile >= bounds[2]) & (tile < bounds[3])

    @pl.when(active & whole)
    def _():
        one_tile(False)

    @pl.when(active & jnp.logical_not(whole))
    def _():
        one_tile(True)

    @pl.when(step == pl.num_programs(0) - 1)
    def _():
        for head in range(heads):
            out_ref[:, head * HD:(head + 1) * HD] = (
                acc[head][:, :HD] / acc[head][:, HD:]
            ).astype(out_ref.dtype)


def attention(queries, keys, values, row_start, row_end):
    rows, width = queries.shape
    tiles = keys.shape[0] // TILE
    low = jnp.min(row_start) // TILE
    high = (jnp.max(row_end) + TILE - 1) // TILE
    whole_low = (jnp.max(row_start) + TILE - 1) // TILE
    whole_high = jnp.min(row_end) // TILE
    bounds = jnp.stack([low, high, whole_low, whole_high]).astype(jnp.int32)

    def kv_map(step, bounds):
        return (jnp.minimum(bounds[0] + step, bounds[1] - 1), 0)

    def fixed(step, bounds):
        return (0, 0)

    return pl.pallas_call(
        attend_kernel,
        out_shape=jax.ShapeDtypeStruct((rows, width), jnp.bfloat16),
        grid_spec=pltpu.PrefetchScalarGridSpec(
            num_scalar_prefetch=1,
            grid=(tiles,),
            in_specs=[
                pl.BlockSpec((rows, width), fixed),
                pl.BlockSpec((rows, 1), fixed),
                pl.BlockSpec((rows, 1), fixed),
                pl.BlockSpec((TILE, width), kv_map),
                pl.BlockSpec((TILE, width), kv_map),
            ],
            out_specs=pl.BlockSpec((rows, width), fixed),
            scratch_shapes=[
                pltpu.VMEM((width // HD, rows, 2 * HD), jnp.float32),
                pltpu.VMEM((width // HD, rows, HD), jnp.float32),
            ],
        ),
        compiler_params=pltpu.CompilerParams(vmem_limit_bytes=40 << 20),
        name="attend",
    )(bounds, queries, row_start[:, None], row_end[:, None], keys, values)


def per_device(
    tokens, queries, key_rows, value_rows, clip_ids, causal, modulation, w_mlp, w_attn_out, w_mlp_out
):
    local_rows = queries.shape[0]
    tp_size = lax.axis_size("tp")
    clips = causal.shape[0]
    first_row = lax.axis_index("ctx") * local_rows
    own_pos = first_row + jnp.arange(local_rows, dtype=jnp.int32)
    own_ids = lax.dynamic_slice_in_dim(clip_ids, first_row, local_rows)
    key_all = lax.all_gather(key_rows, "ctx", axis=0, tiled=True)
    value_all = lax.all_gather(value_rows, "ctx", axis=0, tiled=True)

    numbers = jnp.arange(clips, dtype=jnp.int32)
    clip_start = jnp.sum((clip_ids[None, :] < numbers[:, None]).astype(jnp.int32), axis=1)
    clip_end = jnp.sum((clip_ids[None, :] <= numbers[:, None]).astype(jnp.int32), axis=1)
    mine = own_ids[:, None] == numbers[None, :]
    row_start = jnp.sum(jnp.where(mine, clip_start[None, :], 0), axis=1)
    row_end = jnp.sum(jnp.where(mine, clip_end[None, :], 0), axis=1)
    row_causal = jnp.sum(jnp.where(mine, causal[None, :], 0), axis=1)
    row_end = jnp.where(row_causal == 0, row_end, own_pos + 1)

    whole_rows = lax.all_gather(tokens, "tp", axis=1, tiled=True)
    token_values = whole_rows.astype(jnp.float32)
    row_mean = jnp.mean(token_values, axis=1, keepdims=True)
    centred = token_values - row_mean
    row_var = jnp.mean(centred * centred, axis=1, keepdims=True)
    normed = centred * lax.rsqrt(row_var + eps_norm)
    shift_rows = pick_rows(own_ids, modulation[0])
    scale_rows = pick_rows(own_ids, modulation[1])
    modulated = (normed * (1.0 + scale_rows) + shift_rows).astype(jnp.bfloat16)
    hidden = jax.nn.gelu(
        jnp.dot(modulated, w_mlp, preferred_element_type=jnp.float32), approximate=True
    ).astype(jnp.bfloat16)

    attended = attention(queries, key_all, value_all, row_start, row_end)
    part = jnp.dot(attended, w_attn_out, preferred_element_type=jnp.float32) + jnp.dot(
        hidden, w_mlp_out, preferred_element_type=jnp.float32
    )
    branch = lax.psum_scatter(
        part.astype(jnp.bfloat16), "tp", scatter_dimension=0, tiled=True
    ).astype(jnp.float32)
    share_rows = local_rows // tp_size
    first_share = lax.axis_index("tp") * share_rows
    share_ids = lax.dynamic_slice_in_dim(own_ids, first_share, share_rows)
    residual = lax.dynamic_slice_in_dim(whole_rows, first_share, share_rows, 0).astype(jnp.float32)
    return residual + pick_rows(share_ids, modulation[2]) * branch


def solution(mesh):
    in_specs = (
        P("ctx", "tp"), P("ctx", "tp"), P("ctx", "tp"), P("ctx", "tp"),
        P(), P(), P(), P(None, "tp"), P("tp", None), P("tp", None),
    )
    out_specs = P(("ctx", "tp"), None)
    return jax.shard_map(
        per_device, mesh=mesh, in_specs=in_specs, out_specs=out_specs, check_vma=False
    )
```

time: 496 us -> 364 us (0.73)
  matrix products: 73.8 us -> 15 us
  other arithmetic: 55.2 us -> 10.9 us
  local copies, waits for them, and re-layouts: 34.7 us -> 6.92 us
  waiting for transfers between devices: 308 us -> 287 us
  Pallas kernels: 0 us -> 19.3 us
  between operations: 13.2 us -> 19.6 us
  loops' own time: 5.58 us -> 0 us
    dot_general x19 -> x0, matrix products: 56.9 us -> none  [the longest x8 26.6 us: attend(): jnp.einsum('ihd,jhd->hij', query_tile, key_tile, preferred_element_type=j...]
    dynamic_slice x25 -> x0, local copies, waits for them, and re-layouts: 29.4 us -> none  [the longest x8 11.9 us: one_tile(): lax.dynamic_slice_in_dim(value_piece, offset, tile_rows, 0)]
    reduce_sum x9 -> x2, other arithmetic: 31.1 us -> 1.8 us  [the longest x1 1.04 us: per_device(): jnp.sum((clip_ids[None, :] < numbers[:, None]).astype(jnp.int32), axis=1)]
    reduce_scatter x1, waiting for transfers between devices: 126 us -> 101 us  [per_device(): lax.psum_scatter(part.astype(jnp.bfloat16), 'tp', scatter_dimension=0, ti...]
    pallas_call x0 -> x1, Pallas kernels: none -> 19.3 us  [attention(): pl.pallas_call(attend_kernel, out_shape=jax.ShapeDtypeStruct((rows, width...]
    and x8 -> x0, other arithmetic: 8.77 us -> none  [visible(): return same_clip & ((query_causal[:, None] == 0) | earlier)]
    another operation x1 -> x0, loops' own time: 5.58 us -> none  [per_device(): lax.scan(one_tile, carry_state, jnp.arange(piece_rows // tile_rows, dtype...]
  transfers between devices with their start and end apart: 4 -> 4, of which waited for: 4 -> 4; matrix products, arithmetic and copies ran while one was open for 9% -> 6% of each run, Pallas kernels for 0% -> 0%
where the time goes in v1:
time: 364 us; the launch traced here: 359 us
  waiting for transfers between devices  287 us (79%)
  between operations  19.6 us (5%)
  Pallas kernels  19.3 us (5%)
  matrix products  15 us (4%)
  other arithmetic  10.9 us (3%)
  local copies, waits for them, and re-layouts  6.92 us (2%)
    reduce_scatter x1, waiting for transfers between devices, per_device(): lax.psum_scatter(part.astype(jnp.bfloat16), 'tp', scatter_dimension=0, ti...  101 us
    all_gather x1, waiting for transfers between devices, per_device(): whole_rows = lax.all_gather(tokens, 'tp', axis=1, tiled=True)  67.8 us
    all_gather x1, waiting for transfers between devices, per_device(): value_all = lax.all_gather(value_rows, 'ctx', axis=0, tiled=True)  67.6 us
    all_gather x1, waiting for transfers between devices, per_device(): key_all = lax.all_gather(key_rows, 'ctx', axis=0, tiled=True)  48.9 us
    pallas_call x1, Pallas kernels, attention(): pl.pallas_call(attend_kernel, out_shape=jax.ShapeDtypeStruct((rows, width...  19.3 us
    dot_general x1, matrix products, per_device(): jnp.dot(hidden, w_mlp_out, preferred_element_type=jnp.float32)  12.8 us
  transfers between devices with their start and end apart: 4, of which 4 were waited for; matrix products, arithmetic and copies ran while one was open for 6% of the time, Pallas kernels for 0%

profile of v1, /device:TPU:112, one launch (start us, length us, event | category | flops | bytes accessed | tf_op | source)
XLA Modules:
  0.0 359.3 jit_solution(4784418143578761220)
XLA Ops:
  6.5 0.7 all-gather.4.cloned.1.call-update
  7.3 0.7 all-gather.6.cloned.1.call-update
  8.1 0.7 all-gather.8.cloned.1.call-update
  8.8 0.8 broadcast_compare_fusion.1
  9.6 1.0 convert_reduce_fusion.2
  10.6 0.8 select_reduce_fusion.2
  11.4 0.7 fusion.29
  18.4 0.1 broadcast_in_dim.218.start_ref
  18.6 0.1 pad_add_fusion.bounds
  18.6 0.2 reshape_select_fusion.end_ref
  18.8 1.2 fusion.36
  20.1 67.8 %all-gather.4.cloned.1.call-done = bf16[384,3072]{1,0:T(8,128)(2,1)} async-done(((bf16[384,384]{1,0:T(8,128)(2,1)}), bf16[384,3072]{1,0:T(8,128)(2,1)}) %all-gather.4.cloned.1.call-update) | async-done | bytes 2359312 | tf_op jit(solution)/shard_map/all_gather | solution.py:141
  87.8 2.1 convert_reduce_fusion
  89.9 2.4 fusion.2
  92.3 12.8 %fusion.22 = f32[384,3072]{1,0:T(8,128)} fusion(bf16[768,3072]{1,0:T(8,128)(2,1)} %param.19, bf16[3072,768]{1,0:T(8,128)(2,1)} %param.17, bf16[384,3072]{1,0:T(8,128)(2,1)} %all-gather.4.cloned.1.call-done, f32[3072]{0:T(1024)S(1)} %bitcast.30, f32[3072]{0:T(1024)S(1)} %bitcast.31, f32[3072]{0:T(1024)S(1)} %bitcast.24, f32[3072]{0:T(1024)S(1)} %bitcast.25, ...), kind=kOutput, calls=%fused_computation.22 | convolution fusion | flops 3641868288 | bytes 16617600 | tf_op jit(solution)/shard_map/dot_general | solution.py:155
  105.1 48.9 %all-gather.6.cloned.1.call-done.k_ref = bf16[12288,256]{1,0:T(8,128)(2,1)} async-done(((bf16[384,256]{1,0:T(8,128)(2,1)}), bf16[12288,256]{1,0:T(8,128)(2,1)}) %all-gather.6.cloned.1.call-update) | async-done | bytes 6291472 | tf_op jit(solution)/shard_map/all_gather | solution.py:129
  154.0 67.6 %all-gather.8.cloned.1.call-done.v_ref = bf16[12288,256]{1,0:T(8,128)(2,1)} async-done(((bf16[384,256]{1,0:T(8,128)(2,1)}), bf16[12288,256]{1,0:T(8,128)(2,1)}) %all-gather.8.cloned.1.call-update) | async-done | bytes 6291472 | tf_op jit(solution)/shard_map/all_gather | solution.py:130
  221.6 2.8 copy-done.1
  224.4 2.8 copy-done.2
  227.1 19.3 %attend.1 = bf16[384,256]{1,0:T(8,128)(2,1)S(1)} custom-call(s32[4]{0:T(128)S(1)} %pad_add_fusion.bounds, bf16[384,256]{1,0:T(8,128)(2,1)S(1)} %copy-done.3, s32[384,1]{1,0:T(8,128)S(1)} %broadcast_in_dim.218.start_ref, s32[384,1]{1,0:T(8,128)S(1)} %reshape_select_fusion.end_ref, bf16[12288,256]{1,0:T(8,128)(2,1)S(1)} %copy-done.1, ...), custom_call_target="tpu_custom_call" | custom-call | tf_op jit(solution)/shard_map/attend/pallas_call | solution.py:96
  246.5 2.3 add_convert_fusion
  248.8 0.8 broadcast_compare_fusion.6
  249.6 101.1 %reduce-scatter.2.cloned.1.call-done = bf16[48,3072]{1,0:T(8,128)(2,1)} async-done(((bf16[384,3072]{1,0:T(8,128)(2,1)}), bf16[48,3072]{1,0:T(8,128)(2,1)}) %reduce-scatter.2.cloned.1.call-update) | async-done | bytes 294928 | tf_op jit(solution)/shard_map/reduce_scatter | solution.py:158
  350.7 2.1 multiply_add_fusion
  (16 shorter events, 0.2 us)
Async XLA Ops:
  6.5 239.9 %copy-start = (bf16[256,3072]{1,0:T(8,128)(2,1)S(1)}, bf16[256,3072]{1,0:T(8,128)(2,1)}, u32[]{:S(2)}) copy-start(bf16[256,3072]{1,0:T(8,128)(2,1)} %param.18) | copy-start | bytes 4718596
  6.5 81.3 %all-gather.4.cloned.1.call-start = ((), (), s32[]{:S(2)}) async-start(), calls=%async_computation.1 | async-start | bytes 2654208 | tf_op jit(solution)/shard_map/all_gather | solution.py:141
  7.3 146.7 %all-gather.6.cloned.1.call-start = ((), (), s32[]{:S(2)}) async-start(), calls=%async_computation.2 | async-start | bytes 6488064 | tf_op jit(solution)/shard_map/all_gather | solution.py:129
  8.0 213.6 %all-gather.8.cloned.1.call-start = ((), (), s32[]{:S(2)}) async-start(), calls=%async_computation.3 | async-start | bytes 6488064 | tf_op jit(solution)/shard_map/all_gather | solution.py:130
  8.7 341.9 %reduce-scatter.2.cloned.1.call-start = ((), (), s32[]{:S(2)}) async-start(), calls=%async_computation.4 | async-start | bytes 2654208 | tf_op jit(solution)/shard_map/reduce_scatter | solution.py:158
  92.3 129.3 %copy-start.3 = (bf16[384,256]{1,0:T(8,128)(2,1)S(1)}, bf16[384,256]{1,0:T(8,128)(2,1)}, u32[]{:S(2)}) copy-start(bf16[384,256]{1,0:T(8,128)(2,1)} %q_ref.1) | copy-start | bytes 589828
  221.6 2.8 copy-start.1
  224.3 2.8 copy-start.2
  227.1 19.4 %copy-start.4 = (f32[384,3072]{1,0:T(8,128)S(1)}, f32[384,3072]{1,0:T(8,128)}, u32[]{:S(2)}) copy-start(f32[384,3072]{1,0:T(8,128)} %fusion.22) | copy-start | bytes 14155780
Sparse Core Ops, SparseCore 0:
  9.8 77.9 all-gather.3
  89.7 64.2 all-gather.5
  155.9 65.6 all-gather.7
  248.9 101.7 reduce-scatter.1

commit v2 on v1

--- a/solution.py
+++ b/solution.py
@@ -1,4 +1,3 @@
-import functools
 import math
 
 import jax
@@ -113,8 +112,238 @@
             ],
         ),
         compiler_params=pltpu.CompilerParams(vmem_limit_bytes=40 << 20),
+        cost_estimate=pl.CostEstimate(
+            flops=8 * rows * keys.shape[0] * width,
+            bytes_accessed=4 * keys.shape[0] * width,
+            transcendentals=rows * keys.shape[0] * width // HD,
+        ),
         name="attend",
     )(bounds, queries, row_start[:, None], row_end[:, None], keys, values)
+
+
+def remote(src, dst, send_sem, recv_sem, where):
+    return pltpu.make_async_remote_copy(
+        src_ref=src, dst_ref=dst, send_sem=send_sem, recv_sem=recv_sem,
+        device_id=where, device_id_type=pl.DeviceIdType.MESH,
+    )
+
+
+def greet(places):
+    barrier = pltpu.get_barrier_semaphore()
+    for place in places:
+        pl.semaphore_signal(
+            barrier, inc=1, device_id=place, device_id_type=pl.DeviceIdType.MESH
+        )
+    pl.semaphore_wait(barrier, len(places))
+
+
+Y, Z, CORES = 4, 4, 2
+KV_COPIES = 2 * (Z - 1) + 6 * Z + 2 * Y * Z
+
+
+def gather_kernel(keys, values, key_all, value_all, send, recv, local):
+    rows = keys.shape[0]
+    me = lax.axis_index("ctx")
+    y, z, core = me // (Z * CORES), me // CORES % Z, me % CORES
+    pair = (key_all, value_all)
+    own = (keys, values)
+
+    def index(dy, dz, flip=False):
+        other = 1 - core if flip else core
+        return ((y + dy + Y) % Y * Z + (z + dz + Z) % Z) * CORES + other
+
+    def slot(which, dy, dz, flip=False):
+        start = pl.multiple_of(index(dy, dz, flip) * rows, rows)
+        return pair[which].at[pl.ds(start, rows)]
+
+    def at(dy, dz, flip=False):
+        return {"ctx": index(dy, dz, flip)}
+
+    greet([at(0, d) for d in range(1, Z)] + [at(1, 0), at(-1, 0), at(0, 0, True)])
+    started = []
+    made = [0]
+
+    def make(src, which, owner, target):
+        number = made[0]
+        made[0] += 1
+        copy = remote(
+            src, slot(which, *owner), send.at[number], recv.at[number], at(*target)
+        )
+        copy.start()
+        started.append(copy)
+        return copy
+
+    stay = [pltpu.make_async_copy(own[w], slot(w, 0, 0), local.at[w]) for w in (0, 1)]
+    for copy in stay:
+        copy.start()
+    near = [[None] * 4 for _ in range(Z)]
+    far = [[None] * 2 for _ in range(Z)]
+    to_z = [[None] * 2 for _ in range(Z)]
+    to_core = []
+
+    def spread(dz):
+        for w in (0, 1):
+            src = own[w] if dz == 0 else slot(w, 0, dz)
+            near[dz][w] = make(src, w, (0, dz), (1, 0))
+            near[dz][2 + w] = make(src, w, (0, dz), (-1, 0))
+            to_core.append(make(src, w, (0, dz), (0, 0, True)))
+
+    def relay(dz):
+        near[dz][0].wait_recv()
+        far[dz][0] = make(slot(0, -1, dz), 0, (-1, dz), (1, 0))
+        near[dz][3].wait_recv()
+        far[dz][1] = make(slot(1, 1, dz), 1, (1, dz), (-1, 0))
+        near[dz][1].wait_recv()
+        near[dz][2].wait_recv()
+        for w in (0, 1):
+            for dy in (-1, 1):
+                to_core.append(make(slot(w, dy, dz), w, (dy, dz), (0, 0, True)))
+
+    def finish(dz):
+        for w in (0, 1):
+            far[dz][w].wait_recv()
+            to_core.append(make(slot(w, 2, dz), w, (2, dz), (0, 0, True)))
+
+    for d in (1, 3, 2):
+        for w in (0, 1):
+            to_z[Z - d][w] = make(own[w], w, (0, 0), (0, d))
+    spread(0)
+    order = (0, 1, 3, 2)
+    for i, dz in enumerate(order):
+        if i > 0:
+            for w in (0, 1):
+                to_z[dz][w].wait_recv()
+            spread(dz)
+            relay(order[i - 1])
+        if i > 1:
+            finish(order[i - 2])
+    relay(order[Z - 1])
+    finish(order[Z - 2])
+    finish(order[Z - 1])
+    for copy in to_core:
+        copy.wait_recv()
+    for copy in started:
+        copy.wait_send()
+    for copy in stay:
+        copy.wait()
+
+
+def gather_rows(keys, values, devices):
+    rows, width = keys.shape
+    hbm = pl.BlockSpec(memory_space=pl.ANY)
+    whole = jax.ShapeDtypeStruct((rows * devices, width), keys.dtype)
+    return pl.pallas_call(
+        gather_kernel,
+        out_shape=(whole, whole),
+        in_specs=[hbm, hbm],
+        out_specs=(hbm, hbm),
+        scratch_shapes=[
+            pltpu.SemaphoreType.DMA((KV_COPIES,)),
+            pltpu.SemaphoreType.DMA((KV_COPIES,)),
+            pltpu.SemaphoreType.DMA((2,)),
+        ],
+        compiler_params=pltpu.CompilerParams(collective_id=0, has_side_effects=True),
+        cost_estimate=pl.CostEstimate(flops=0, bytes_accessed=150_000_000, transcendentals=0),
+        name="gather_kv",
+    )(keys, values)
+
+
+X, HI, CHUNKS = 4, 2, 4
+
+
+def reduce_kernel(part, out, held, relayed, outgoing, incoming, sums, send, recv):
+    rows = part.shape[0] // (X * HI)
+    wide = part.shape[1] // CHUNKS
+    me = lax.axis_index("tp")
+    x, hi = me // HI, me % HI
+    right = {"tp": (x + 1) % X * HI + hi}
+    left = {"tp": (x + X - 1) % X * HI + hi}
+    across = {"tp": x * HI + 1 - hi}
+    greet([left, right, across])
+
+    def piece(dx, first, count, chunk):
+        start = pl.multiple_of(((x + dx) % X * HI + first) * rows, rows)
+        return part.at[pl.ds(start, count * rows), pl.ds(chunk * wide, wide)]
+
+    def cols(chunk):
+        return slice(chunk * wide, (chunk + 1) * wide)
+
+    def copy(src, dst, chunk, kind, where):
+        made = remote(src, dst, send.at[chunk, kind], recv.at[chunk, kind], where)
+        made.start()
+        return made
+
+    copies = [[None] * 7 for _ in range(CHUNKS)]
+
+    def begin(c):
+        mine = copies[c]
+        mine[2] = copy(piece(2, 0, 1, c), relayed.at[0, c], c, 2, right)
+        mine[3] = copy(piece(2, 1, 1, c), relayed.at[1, c], c, 3, left)
+        mine[0] = copy(piece(1, 0, 2, c), held.at[0, c], c, 0, right)
+        mine[1] = copy(piece(3, 0, 2, c), held.at[1, c], c, 1, left)
+
+    def forward(c):
+        mine = copies[c]
+        mine[2].wait_recv()
+        mine[4] = copy(relayed.at[0, c], held.at[2, c, pl.ds(0, rows)], c, 4, right)
+        mine[3].wait_recv()
+        mine[5] = copy(relayed.at[1, c], held.at[2, c, pl.ds(rows, rows)], c, 5, left)
+
+    def total(c, half):
+        start = pl.multiple_of(half * rows, rows)
+        own = pl.multiple_of((x * HI + half) * rows, rows)
+        result = part[pl.ds(own, rows), cols(c)].astype(jnp.float32)
+        for source in range(3):
+            result += held[source, c, pl.ds(start, rows)].astype(jnp.float32)
+        return result
+
+    def combine(c):
+        mine = copies[c]
+        for kind in (0, 1, 4, 5):
+            mine[kind].wait_recv()
+        outgoing[c] = total(c, 1 - hi).astype(jnp.bfloat16)
+        sums[c] = total(c, hi)
+        mine[6] = copy(outgoing.at[c], incoming.at[c], c, 6, across)
+
+    for c in range(CHUNKS):
+        begin(c)
+    for c in range(CHUNKS):
+        forward(c)
+        if c > 0:
+            combine(c - 1)
+    combine(CHUNKS - 1)
+    for c in range(CHUNKS):
+        copies[c][6].wait_recv()
+        out[:, cols(c)] = sums[c] + incoming[c].astype(jnp.float32)
+    for mine in copies:
+        for made in mine:
+            made.wait_send()
+
+
+def reduce_rows(part):
+    rows, width = part.shape[0] // (X * HI), part.shape[1]
+    wide = width // CHUNKS
+    vmem = pl.BlockSpec(memory_space=pltpu.VMEM)
+    return pl.pallas_call(
+        reduce_kernel,
+        out_shape=jax.ShapeDtypeStruct((rows, width), jnp.float32),
+        in_specs=[vmem],
+        out_specs=vmem,
+        scratch_shapes=[
+            pltpu.VMEM((3, CHUNKS, HI * rows, wide), jnp.bfloat16),
+            pltpu.VMEM((2, CHUNKS, rows, wide), jnp.bfloat16),
+            pltpu.VMEM((CHUNKS, rows, wide), jnp.bfloat16),
+            pltpu.VMEM((CHUNKS, rows, wide), jnp.bfloat16),
+            pltpu.VMEM((CHUNKS, rows, wide), jnp.float32),
+            pltpu.SemaphoreType.DMA((CHUNKS, 7)),
+            pltpu.SemaphoreType.DMA((CHUNKS, 7)),
+        ],
+        compiler_params=pltpu.CompilerParams(
+            collective_id=1, has_side_effects=True, vmem_limit_bytes=24 << 20
+        ),
+        cost_estimate=pl.CostEstimate(flops=0, bytes_accessed=100_000_000, transcendentals=0),
+        name="reduce_branch",
+    )(part)
 
 
 def per_device(
@@ -126,8 +355,7 @@
     first_row = lax.axis_index("ctx") * local_rows
     own_pos = first_row + jnp.arange(local_rows, dtype=jnp.int32)
     own_ids = lax.dynamic_slice_in_dim(clip_ids, first_row, local_rows)
-    key_all = lax.all_gather(key_rows, "ctx", axis=0, tiled=True)
-    value_all = lax.all_gather(value_rows, "ctx", axis=0, tiled=True)
+    key_all, value_all = gather_rows(key_rows, value_rows, lax.axis_size("ctx"))
 
     numbers = jnp.arange(clips, dtype=jnp.int32)
     clip_start = jnp.sum((clip_ids[None, :] < numbers[:, None]).astype(jnp.int32), axis=1)
@@ -155,9 +383,7 @@
     part = jnp.dot(attended, w_attn_out, preferred_element_type=jnp.float32) + jnp.dot(
         hidden, w_mlp_out, preferred_element_type=jnp.float32
     )
-    branch = lax.psum_scatter(
-        part.astype(jnp.bfloat16), "tp", scatter_dimension=0, tiled=True
-    ).astype(jnp.float32)
+    branch = reduce_rows(part.astype(jnp.bfloat16))
     share_rows = local_rows // tp_size
     first_share = lax.axis_index("tp") * share_rows
     share_ids = lax.dynamic_slice_in_dim(own_ids, first_share, share_rows)

time: 364 us -> 200 us (0.55); the launches traced: 359 us -> 199 us
  waiting for transfers between devices: 287 us -> 0.73 us
  Pallas kernels: 19.3 us -> 144 us
    pallas_call x0 -> x2, Pallas kernels: none -> 125 us  [the longest x1 77.6 us: gather_rows(): pl.pallas_call(gather_kernel, out_shape=(whole, whole), in_specs=[hbm, hb...]
    all_gather x2 -> x0, waiting for transfers between devices: 116 us -> none  [the longest x1 67.6 us: per_device(): value_all = lax.all_gather(value_rows, 'ctx', axis=0, tiled=True)]
    reduce_scatter x1 -> x0, waiting for transfers between devices: 101 us -> none  [per_device(): lax.psum_scatter(part.astype(jnp.bfloat16), 'tp', scatter_dimension=0, ti...]
    all_gather x1, waiting for transfers between devices: 67.8 us -> 0.02 us  [per_device(): whole_rows = lax.all_gather(tokens, 'tp', axis=1, tiled=True)]
  transfers between devices with their start and end apart: 4 -> 1, of which waited for: 4 -> 0; matrix products, arithmetic and copies ran while one was open for 6% -> 3% of each run, Pallas kernels for 0% -> 49%
where the time goes in v2:
time: 200 us; the launch traced here: 199 us
  Pallas kernels  144 us (72%)
  between operations  20.1 us (10%)
  matrix products  15.9 us (8%)
  other arithmetic  10.8 us (5%)
  local copies, waits for them, and re-layouts  7.92 us (4%)
    pallas_call x1, Pallas kernels, gather_rows(): pl.pallas_call(gather_kernel, out_shape=(whole, whole), in_specs=[hbm, hb...  77.6 us
    pallas_call x1, Pallas kernels, reduce_rows(): pl.pallas_call(reduce_kernel, out_shape=jax.ShapeDtypeStruct((rows, width...  47.2 us
    pallas_call x1, Pallas kernels, attention(): pl.pallas_call(attend_kernel, out_shape=jax.ShapeDtypeStruct((rows, width...  19.2 us
    dot_general x1, matrix products, per_device(): jnp.dot(hidden, w_mlp_out, preferred_element_type=jnp.float32)  12.8 us
    unnamed x8, local copies, waits for them, and re-layouts  6.49 us
  transfers between devices with their start and end apart: 1, of which 0 were waited for; matrix products, arithmetic and copies ran while one was open for 3% of the time, Pallas kernels for 49%

profile of v2, /device:TPU:112, one launch (start us, length us, event | category | flops | bytes accessed | tf_op | source)
XLA Modules:
  0.0 199.5 jit_solution(10585180822104283067)
XLA Ops:
  6.5 0.0 copy-start
  6.5 0.0 all-gather.2.cloned.1.call-start
  6.5 0.7 all-gather.2.cloned.1.call-update
  7.3 0.8 broadcast_compare_fusion.1
  8.0 1.0 convert_reduce_fusion.2
  9.1 0.8 select_reduce_fusion.2
  9.8 0.7 fusion.29
  17.1 0.1 broadcast_in_dim.218.start_ref
  17.3 77.6 %gather_kv.1 = (bf16[12288,256]{1,0:T(8,128)(2,1)}, bf16[12288,256]{1,0:T(8,128)(2,1)}) custom-call(bf16[384,256]{1,0:T(8,128)(2,1)} %keys.1, bf16[384,256]{1,0:T(8,128)(2,1)} %values.1), custom_call_target="tpu_custom_call" | custom-call | bytes 150000000 | tf_op jit(solution)/shard_map/gather_kv/pallas_call | solution.py:235
  94.9 0.1 pad_add_fusion.bounds
  95.0 0.8 broadcast_compare_fusion.6
  95.7 0.2 reshape_select_fusion.end_ref
  95.9 1.3 fusion.36
  97.3 2.8 %copy-done.1 = bf16[12288,256]{1,0:T(8,128)(2,1)S(1)} copy-done((bf16[12288,256]{1,0:T(8,128)(2,1)S(1)}, bf16[12288,256]{1,0:T(8,128)(2,1)}, u32[]{:S(2)}) %copy-start.1) | copy-done | bytes 6291480
  100.0 2.8 %copy-done.2 = bf16[12288,256]{1,0:T(8,128)(2,1)S(1)} copy-done((bf16[12288,256]{1,0:T(8,128)(2,1)S(1)}, bf16[12288,256]{1,0:T(8,128)(2,1)}, u32[]{:S(2)}) %copy-start.2) | copy-done | bytes 6291480
  102.8 0.9 copy-done.3
  103.7 19.2 %attend.1 = bf16[384,256]{1,0:T(8,128)(2,1)S(1)} custom-call(s32[4]{0:T(128)S(1)} %pad_add_fusion.bounds, bf16[384,256]{1,0:T(8,128)(2,1)S(1)} %copy-done.3, s32[384,1]{1,0:T(8,128)S(1)} %broadcast_in_dim.218.start_ref, s32[384,1]{1,0:T(8,128)S(1)} %reshape_select_fusion.end_ref, bf16[12288,256]{1,0:T(8,128)(2,1)S(1)} %copy-done.1, ...), custom_call_target="tpu_custom_call" | custom-call | flops 9663676416 | bytes 12582912 | tf_op jit(solution)/shard_map/attend/pallas_call | solution.py:95
  123.0 0.0 all-gather.2.cloned.1.call-done
  123.0 2.1 %convert_reduce_fusion = f32[384]{0:T(512)S(1)} fusion(bf16[384,3072]{1,0:T(8,128)(2,1)} %all-gather.2.cloned.1.call-done), kind=kLoop, calls=%fused_computation.1 | loop fusion | flops 2358912 | bytes 2360832 | tf_op jit(solution)/shard_map/reduce_sum | solution.py:371
  125.1 2.4 %fusion.2 = f32[384]{0:T(512)S(1)} fusion(bf16[384,3072]{1,0:T(8,128)(2,1)} %all-gather.2.cloned.1.call-done, f32[384]{0:T(512)S(1)} %broadcast_multiply_fusion), kind=kLoop, calls=%fused_computation.4 | loop fusion | flops 4718208 | bytes 2362368 | tf_op jit(solution)/shard_map/reduce_sum | solution.py:373
  127.5 12.8 %fusion.22 = f32[384,3072]{1,0:T(8,128)} fusion(bf16[768,3072]{1,0:T(8,128)(2,1)} %param.19, bf16[3072,768]{1,0:T(8,128)(2,1)} %param.17, bf16[384,3072]{1,0:T(8,128)(2,1)} %all-gather.2.cloned.1.call-done, f32[3072]{0:T(1024)S(1)} %bitcast.30, f32[3072]{0:T(1024)S(1)} %bitcast.31, f32[3072]{0:T(1024)S(1)} %bitcast.24, f32[3072]{0:T(1024)S(1)} %bitcast.25, ...), kind=kOutput, calls=%fused_computation.22 | convolution fusion | flops 3641868288 | bytes 16617600 | tf_op jit(solution)/shard_map/dot_general | solution.py:383
  140.3 3.1 %add_convert_fusion.part = bf16[384,3072]{1,0:T(8,128)(2,1)S(1)} fusion(f32[384,3072]{1,0:T(8,128)} %fusion.22, bf16[384,256]{1,0:T(8,128)(2,1)S(1)} %attend.1, bf16[256,3072]{1,0:T(8,128)(2,1)S(1)} %copy-done), kind=kOutput, calls=%fused_computation.8 | convolution fusion | flops 606339072 | bytes 8847360 | tf_op jit(solution)/shard_map/dot_general | solution.py:383
  143.4 47.2 %reduce_branch.1 = f32[48,3072]{1,0:T(8,128)S(1)} custom-call(bf16[384,3072]{1,0:T(8,128)(2,1)S(1)} %add_convert_fusion.part), custom_call_target="tpu_custom_call" | custom-call | bytes 100000000 | tf_op jit(solution)/shard_map/reduce_branch/pallas_call | solution.py:327
  190.6 2.0 multiply_add_fusion
  (7 shorter events, 0.0 us)
Async XLA Ops:
  6.5 133.8 %copy-start = (bf16[256,3072]{1,0:T(8,128)(2,1)S(1)}, bf16[256,3072]{1,0:T(8,128)(2,1)}, u32[]{:S(2)}) copy-start(bf16[256,3072]{1,0:T(8,128)(2,1)} %param.18) | copy-start | bytes 4718596
  6.5 116.5 %all-gather.2.cloned.1.call-start = ((), (), s32[]{:S(2)}) async-start(), calls=%async_computation | async-start | bytes 2654208 | tf_op jit(solution)/shard_map/all_gather | solution.py:369
  97.2 2.8 %copy-start.1 = (bf16[12288,256]{1,0:T(8,128)(2,1)S(1)}, bf16[12288,256]{1,0:T(8,128)(2,1)}, u32[]{:S(2)}) copy-start(bf16[12288,256]{1,0:T(8,128)(2,1)} %get-tuple-element.7.k_ref) | copy-start | bytes 18874372
  100.0 2.8 %copy-start.2 = (bf16[12288,256]{1,0:T(8,128)(2,1)S(1)}, bf16[12288,256]{1,0:T(8,128)(2,1)}, u32[]{:S(2)}) copy-start(bf16[12288,256]{1,0:T(8,128)(2,1)} %get-tuple-element.8.v_ref) | copy-start | bytes 18874372
  102.8 0.9 copy-start.3
Sparse Core Ops, SparseCore 0:
  9.8 74.9 all-gather.1

commit v3 on v2

--- a/solution.py
+++ b/solution.py
@@ -20,9 +20,35 @@
     return out
 
 
-def attend_kernel(bounds, q_ref, start_ref, end_ref, k_ref, v_ref, out_ref, acc, peak):
+def interval(table, first, rows):
+    clips = table.shape[0] // 2
+
+    def clip_of(pos):
+        number = jnp.int32(0)
+        for clip in range(clips - 1):
+            number = number + (pos >= table[clip]).astype(jnp.int32)
+        return number
+
+    def start_of(number):
+        return jnp.where(number == 0, 0, table[jnp.maximum(number - 1, 0)])
+
+    low, high = clip_of(first), clip_of(first + rows - 1)
+    end = jnp.where(table[clips + high] == 0, table[high], first + rows)
+    whole_end = jnp.where(table[clips + low] == 0, table[low], first + 1)
+    return start_of(low), end, start_of(high), whole_end
+
+
+def clips_at(positions, clip_end):
+    return jnp.sum((positions[:, None] >= clip_end[None, :-1]).astype(jnp.int32), axis=1)
+
+
+def attend_kernel(table, q_ref, k_ref, v_ref, out_ref, acc, peak, edges):
     step = pl.program_id(0)
-    tile = bounds[0] + step
+    rows = q_ref.shape[0]
+    clips = table.shape[0] // 2
+    first = lax.axis_index("ctx") * rows
+    some_low, some_high, whole_low, whole_high = interval(table, first, rows)
+    tile = some_low // TILE + step
     factor = math.log2(math.e) / math.sqrt(HD)
     heads = q_ref.shape[1] // HD
 
@@ -30,12 +56,22 @@
     def _():
         acc[...] = jnp.zeros_like(acc)
         peak[...] = jnp.full_like(peak, neg_large)
+        pos = first + lax.broadcasted_iota(jnp.int32, (rows, HD), 0)
+        start = jnp.zeros_like(pos)
+        end = jnp.where(table[clips] == 0, table[0], pos + 1)
+        for clip in range(1, clips):
+            later = pos >= table[clip - 1]
+            start = jnp.where(later, table[clip - 1], start)
+            end = jnp.where(
+                later, jnp.where(table[clips + clip] == 0, table[clip], pos + 1), end
+            )
+        edges[0] = start
+        edges[1] = end
 
     def one_tile(masked):
-        rows = q_ref.shape[0]
         if masked:
             pos = tile * TILE + lax.broadcasted_iota(jnp.int32, (rows, TILE), 1)
-            allowed = (pos >= start_ref[...]) & (pos < end_ref[...])
+            allowed = (pos >= edges[0][:, :1]) & (pos < edges[1][:, :1])
         ones = jnp.ones((TILE, HD), jnp.bfloat16)
         for head in range(heads):
             cols = slice(head * HD, (head + 1) * HD)
@@ -58,8 +94,8 @@
             acc[head] = acc[head] * jnp.concatenate([shrink, shrink], axis=1) + added
             peak[head] = new
 
-    active = tile < bounds[1]
-    whole = (tile >= bounds[2]) & (tile < bounds[3])
+    active = tile * TILE < some_high
+    whole = (tile * TILE >= whole_low) & ((tile + 1) * TILE <= whole_high)
 
     @pl.when(active & whole)
     def _():
@@ -77,19 +113,15 @@
             ).astype(out_ref.dtype)
 
 
-def attention(queries, keys, values, row_start, row_end):
+def attention(queries, keys, values, table):
     rows, width = queries.shape
     tiles = keys.shape[0] // TILE
-    low = jnp.min(row_start) // TILE
-    high = (jnp.max(row_end) + TILE - 1) // TILE
-    whole_low = (jnp.max(row_start) + TILE - 1) // TILE
-    whole_high = jnp.min(row_end) // TILE
-    bounds = jnp.stack([low, high, whole_low, whole_high]).astype(jnp.int32)
-
-    def kv_map(step, bounds):
-        return (jnp.minimum(bounds[0] + step, bounds[1] - 1), 0)
-
-    def fixed(step, bounds):
+
+    def kv_map(step, table):
+        low, high, _, _ = interval(table, lax.axis_index("ctx") * rows, rows)
+        return (jnp.minimum(low // TILE + step, (high - 1) // TILE), 0)
+
+    def fixed(step, table):
         return (0, 0)
 
     return pl.pallas_call(
@@ -100,8 +132,6 @@
             grid=(tiles,),
             in_specs=[
                 pl.BlockSpec((rows, width), fixed),
-                pl.BlockSpec((rows, 1), fixed),
-                pl.BlockSpec((rows, 1), fixed),
                 pl.BlockSpec((TILE, width), kv_map),
                 pl.BlockSpec((TILE, width), kv_map),
             ],
@@ -109,16 +139,17 @@
             scratch_shapes=[
                 pltpu.VMEM((width // HD, rows, 2 * HD), jnp.float32),
                 pltpu.VMEM((width // HD, rows, HD), jnp.float32),
+                pltpu.VMEM((2, rows, HD), jnp.int32),
             ],
         ),
-        compiler_params=pltpu.CompilerParams(vmem_limit_bytes=40 << 20),
+        compiler_params=pltpu.CompilerParams(vmem_limit_bytes=60 << 20),
         cost_estimate=pl.CostEstimate(
             flops=8 * rows * keys.shape[0] * width,
             bytes_accessed=4 * keys.shape[0] * width,
             transcendentals=rows * keys.shape[0] * width // HD,
         ),
         name="attend",
-    )(bounds, queries, row_start[:, None], row_end[:, None], keys, values)
+    )(table, queries, keys, values)
 
 
 def remote(src, dst, send_sem, recv_sem, where):
@@ -138,10 +169,11 @@
 
 
 Y, Z, CORES = 4, 4, 2
-KV_COPIES = 2 * (Z - 1) + 6 * Z + 2 * Y * Z
-
-
-def gather_kernel(keys, values, key_all, value_all, send, recv, local):
+X, HI = 4, 2
+COPIES = 2 * (Z - 1) + 6 * Z + 2 * Y * Z + 9
+
+
+def gather_kernel(tokens, keys, values, whole, key_all, value_all, send, recv, local):
     rows = keys.shape[0]
     me = lax.axis_index("ctx")
     y, z, core = me // (Z * CORES), me // CORES % Z, me % CORES
@@ -159,21 +191,44 @@
     def at(dy, dz, flip=False):
         return {"ctx": index(dy, dz, flip)}
 
-    greet([at(0, d) for d in range(1, Z)] + [at(1, 0), at(-1, 0), at(0, 0, True)])
+    lead = lax.axis_index("tp")
+    x, hi = lead // HI, lead % HI
+    half, wide = tokens.shape[0] // 2, tokens.shape[1]
+
+    def column(dx, flip=False):
+        return (x + dx + X) % X * HI + (1 - hi if flip else hi)
+
+    def strip(dx, flip=False, part=None):
+        cols = pl.ds(pl.multiple_of(column(dx, flip) * wide, wide), wide)
+        if part is None:
+            return whole.at[:, cols]
+        return whole.at[pl.ds(part * half, half), cols]
+
+    right, left = {"tp": column(1)}, {"tp": column(-1)}
+    across = {"tp": column(0, True)}
+    greet(
+        [at(0, d) for d in range(1, Z)]
+        + [at(1, 0), at(-1, 0), at(0, 0, True), right, left, across]
+    )
     started = []
     made = [0]
 
-    def make(src, which, owner, target):
+    def pass_on(src, dst, where):
         number = made[0]
         made[0] += 1
-        copy = remote(
-            src, slot(which, *owner), send.at[number], recv.at[number], at(*target)
-        )
+        copy = remote(src, dst, send.at[number], recv.at[number], where)
         copy.start()
         started.append(copy)
         return copy
 
+    over = pass_on(tokens, strip(0), across)
+    sides = [pass_on(tokens, strip(0), right), pass_on(tokens, strip(0), left)]
+
+    def make(src, which, owner, target):
+        return pass_on(src, slot(which, *owner), at(*target))
+
     stay = [pltpu.make_async_copy(own[w], slot(w, 0, 0), local.at[w]) for w in (0, 1)]
+    stay.append(pltpu.make_async_copy(tokens, strip(0), local.at[2]))
     for copy in stay:
         copy.start()
     near = [[None] * 4 for _ in range(Z)]
@@ -208,6 +263,16 @@
         for w in (0, 1):
             to_z[Z - d][w] = make(own[w], w, (0, 0), (0, d))
     spread(0)
+
+    def tokens_far(arrived, flip):
+        for copy in arrived:
+            copy.wait_recv()
+        return [
+            pass_on(strip(-1, flip, 0), strip(-1, flip, 0), right),
+            pass_on(strip(1, flip, 1), strip(1, flip, 1), left),
+        ]
+
+    ends = tokens_far(sides, False)
     order = (0, 1, 3, 2)
     for i, dz in enumerate(order):
         if i > 0:
@@ -215,8 +280,15 @@
                 to_z[dz][w].wait_recv()
             spread(dz)
             relay(order[i - 1])
+        if i == 1:
+            over.wait_recv()
+            sides = [pass_on(strip(0, True), strip(0, True), to) for to in (right, left)]
+        if i == 2:
+            ends += tokens_far(sides, True)
         if i > 1:
             finish(order[i - 2])
+    for copy in ends:
+        copy.wait_recv()
     relay(order[Z - 1])
     finish(order[Z - 2])
     finish(order[Z - 1])
@@ -228,27 +300,33 @@
         copy.wait()
 
 
-def gather_rows(keys, values, devices):
+def gather_rows(tokens, keys, values, devices, leads):
     rows, width = keys.shape
     hbm = pl.BlockSpec(memory_space=pl.ANY)
-    whole = jax.ShapeDtypeStruct((rows * devices, width), keys.dtype)
+    vmem = pl.BlockSpec(memory_space=pltpu.VMEM)
+    gathered = jax.ShapeDtypeStruct((rows * devices, width), keys.dtype)
     return pl.pallas_call(
         gather_kernel,
-        out_shape=(whole, whole),
-        in_specs=[hbm, hbm],
-        out_specs=(hbm, hbm),
+        out_shape=(
+            jax.ShapeDtypeStruct((rows, tokens.shape[1] * leads), tokens.dtype),
+            gathered,
+            gathered,
+        ),
+        in_specs=[hbm, hbm, hbm],
+        out_specs=(vmem, hbm, hbm),
         scratch_shapes=[
-            pltpu.SemaphoreType.DMA((KV_COPIES,)),
-            pltpu.SemaphoreType.DMA((KV_COPIES,)),
-            pltpu.SemaphoreType.DMA((2,)),
+            pltpu.SemaphoreType.DMA((COPIES,)),
+            pltpu.SemaphoreType.DMA((COPIES,)),
+            pltpu.SemaphoreType.DMA((3,)),
         ],
-        compiler_params=pltpu.CompilerParams(collective_id=0, has_side_effects=True),
-        cost_estimate=pl.CostEstimate(flops=0, bytes_accessed=150_000_000, transcendentals=0),
-        name="gather_kv",
-    )(keys, values)
-
-
-X, HI, CHUNKS = 4, 2, 4
+        compiler_params=pltpu.CompilerParams(
+            collective_id=0, has_side_effects=True, vmem_limit_bytes=48 << 20
+        ),
+        name="gather_all",
+    )(tokens, keys, values)
+
+
+CHUNKS = 4
 
 
 def reduce_kernel(part, out, held, relayed, outgoing, incoming, sums, send, recv):
@@ -353,20 +431,12 @@
     tp_size = lax.axis_size("tp")
     clips = causal.shape[0]
     first_row = lax.axis_index("ctx") * local_rows
-    own_pos = first_row + jnp.arange(local_rows, dtype=jnp.int32)
-    own_ids = lax.dynamic_slice_in_dim(clip_ids, first_row, local_rows)
-    key_all, value_all = gather_rows(key_rows, value_rows, lax.axis_size("ctx"))
-
+    whole_rows, key_all, value_all = gather_rows(
+        tokens, key_rows, value_rows, lax.axis_size("ctx"), tp_size
+    )
     numbers = jnp.arange(clips, dtype=jnp.int32)
-    clip_start = jnp.sum((clip_ids[None, :] < numbers[:, None]).astype(jnp.int32), axis=1)
     clip_end = jnp.sum((clip_ids[None, :] <= numbers[:, None]).astype(jnp.int32), axis=1)
-    mine = own_ids[:, None] == numbers[None, :]
-    row_start = jnp.sum(jnp.where(mine, clip_start[None, :], 0), axis=1)
-    row_end = jnp.sum(jnp.where(mine, clip_end[None, :], 0), axis=1)
-    row_causal = jnp.sum(jnp.where(mine, causal[None, :], 0), axis=1)
-    row_end = jnp.where(row_causal == 0, row_end, own_pos + 1)
-
-    whole_rows = lax.all_gather(tokens, "tp", axis=1, tiled=True)
+    own_ids = clips_at(first_row + jnp.arange(local_rows, dtype=jnp.int32), clip_end)
     token_values = whole_rows.astype(jnp.float32)
     row_mean = jnp.mean(token_values, axis=1, keepdims=True)
     centred = token_values - row_mean
@@ -379,14 +449,16 @@
         jnp.dot(modulated, w_mlp, preferred_element_type=jnp.float32), approximate=True
     ).astype(jnp.bfloat16)
 
-    attended = attention(queries, key_all, value_all, row_start, row_end)
+    attended = attention(queries, key_all, value_all, jnp.concatenate([clip_end, causal]))
     part = jnp.dot(attended, w_attn_out, preferred_element_type=jnp.float32) + jnp.dot(
         hidden, w_mlp_out, preferred_element_type=jnp.float32
     )
     branch = reduce_rows(part.astype(jnp.bfloat16))
     share_rows = local_rows // tp_size
     first_share = lax.axis_index("tp") * share_rows
-    share_ids = lax.dynamic_slice_in_dim(own_ids, first_share, share_rows)
+    share_ids = clips_at(
+        first_row + first_share + jnp.arange(share_rows, dtype=jnp.int32), clip_end
+    )
     residual = lax.dynamic_slice_in_dim(whole_rows, first_share, share_rows, 0).astype(jnp.float32)
     return residual + pick_rows(share_ids, modulation[2]) * branch
 

time: 200 us -> 178 us (0.89)
  between operations: 20.1 us -> 0.07 us
  Pallas kernels: 144 us -> 151 us
  other arithmetic: 10.8 us -> 5.79 us
  local copies, waits for them, and re-layouts: 7.92 us -> 4.14 us
    pallas_call x1, Pallas kernels: 77.6 us -> 82.9 us  [gather_rows(): pl.pallas_call(gather_kernel, out_shape=(jax.ShapeDtypeStruct((rows, toke...]
    pallas_call x1, Pallas kernels: 19.2 us -> 23.2 us  [attention(): pl.pallas_call(attend_kernel, out_shape=jax.ShapeDtypeStruct((rows, width...]
    unnamed x8 -> x12, local copies, waits for them, and re-layouts: 6.49 us -> 2.82 us
    pallas_call x1, Pallas kernels: 47.2 us -> 44.4 us  [reduce_rows(): pl.pallas_call(reduce_kernel, out_shape=jax.ShapeDtypeStruct((rows, width...]
  transfers between devices with their start and end apart: 1 -> 0, of which waited for: 0 -> 0; matrix products, arithmetic and copies ran while one was open for 3% -> 0% of each run, Pallas kernels for 49% -> 0%
where the time goes in v3:
time: 178 us; the launch traced here: 176 us
  Pallas kernels  151 us (85%)
  matrix products  15.9 us (9%)
  other arithmetic  5.79 us (3%)
  local copies, waits for them, and re-layouts  4.14 us (2%)
    pallas_call x1, Pallas kernels, gather_rows(): pl.pallas_call(gather_kernel, out_shape=(jax.ShapeDtypeStruct((rows, toke...  82.9 us
    pallas_call x1, Pallas kernels, reduce_rows(): pl.pallas_call(reduce_kernel, out_shape=jax.ShapeDtypeStruct((rows, width...  44.4 us
    pallas_call x1, Pallas kernels, attention(): pl.pallas_call(attend_kernel, out_shape=jax.ShapeDtypeStruct((rows, width...  23.2 us
    dot_general x1, matrix products, per_device(): jnp.dot(hidden, w_mlp_out, preferred_element_type=jnp.float32)  12.8 us

profile of v3, /device:TPU:112, one launch (start us, length us, event | category | flops | bytes accessed | tf_op | source)
XLA Modules:
  0.0 176.4 jit_solution(5765174242947195572)
XLA Ops:
  0.0 0.0 copy-start
  0.0 1.1 convert_reduce_fusion.1
  1.1 0.1 convert_reduce_fusion.3
  1.2 1.3 pad_add_fusion.table
  2.6 0.1 convert_reduce_fusion.2
  2.7 1.3 fusion.33
  4.0 0.0 copy-start.2
  4.0 1.0 copy-done.2
  4.9 0.0 copy-start.3
  4.9 0.9 copy-done.3
  5.9 0.9 copy-done.4
  6.8 82.9 %gather_all.1 = (bf16[384,3072]{1,0:T(8,128)(2,1)S(1)}, bf16[12288,256]{1,0:T(8,128)(2,1)}, bf16[12288,256]{1,0:T(8,128)(2,1)}) custom-call(bf16[384,384]{1,0:T(8,128)(2,1)S(1)} %copy-done.2, bf16[384,256]{1,0:T(8,128)(2,1)S(1)} %copy-done.3, bf16[384,256]{1,0:T(8,128)(2,1)S(1)} %copy-done.4), custom_call_target="tpu_custom_call" | custom-call | tf_op jit(solution)/shard_map/gather_all/pallas_call | solution.py:308
  89.7 0.0 copy-start.1
  89.7 23.2 %attend.1 = bf16[384,256]{1,0:T(8,128)(2,1)} custom-call(s32[8]{0:T(128)} %pad_add_fusion.table, bf16[384,256]{1,0:T(8,128)(2,1)} %q_ref.1, bf16[12288,256]{1,0:T(8,128)(2,1)} %get-tuple-element.9.k_ref, bf16[12288,256]{1,0:T(8,128)(2,1)} %get-tuple-element.10.v_ref), custom_call_target="tpu_custom_call" | custom-call | flops 9663676416 | bytes 12582912 | tf_op jit(solution)/shard_map/attend/pallas_call | solution.py:127
  113.0 0.4 convert_reduce_fusion
  113.4 0.0 copy-done.1
  113.4 0.8 fusion.2
  114.1 0.0 copy-start.5
  114.1 12.8 %fusion.22 = f32[384,3072]{1,0:T(8,128)} fusion(bf16[768,3072]{1,0:T(8,128)(2,1)} %param.19, bf16[3072,768]{1,0:T(8,128)(2,1)} %param.17, bf16[384,3072]{1,0:T(8,128)(2,1)} %copy-done.1, f32[3072]{0:T(1024)S(1)} %bitcast.27, f32[3072]{0:T(1024)S(1)} %bitcast.28, f32[3072]{0:T(1024)S(1)} %bitcast.21, f32[3072]{0:T(1024)S(1)} %bitcast.22, ...), kind=kOutput, calls=%fused_computation.22 | convolution fusion | flops 3641868288 | bytes 16617600 | tf_op jit(solution)/shard_map/dot_general | solution.py:453
  126.9 0.0 copy-done
  126.9 0.0 copy-done.5
  126.9 3.1 %add_convert_fusion.part = bf16[384,3072]{1,0:T(8,128)(2,1)S(1)} fusion(f32[384,3072]{1,0:T(8,128)} %fusion.22, bf16[384,256]{1,0:T(8,128)(2,1)S(1)} %copy-done.5, bf16[256,3072]{1,0:T(8,128)(2,1)S(1)} %copy-done), kind=kOutput, calls=%fused_computation.8 | convolution fusion | flops 606339072 | bytes 8847360 | tf_op jit(solution)/shard_map/dot_general | solution.py:453
  130.1 44.4 %reduce_branch.1 = f32[48,3072]{1,0:T(8,128)S(1)} custom-call(bf16[384,3072]{1,0:T(8,128)(2,1)S(1)} %add_convert_fusion.part), custom_call_target="tpu_custom_call" | custom-call | bytes 100000000 | tf_op jit(solution)/shard_map/reduce_branch/pallas_call | solution.py:405
  174.4 2.0 %multiply_add_fusion = f32[48,3072]{1,0:T(8,128)} fusion(f32[48,3072]{1,0:T(8,128)S(1)} %reduce_branch.1, f32[3072]{0:T(1024)S(1)} %bitcast.18, f32[3072]{0:T(1024)S(1)} %bitcast.19, f32[3072]{0:T(1024)S(1)} %bitcast.20, f32[3072]{0:T(1024)S(1)} %bitcast.17, bf16[384,3072]{1,0:T(8,128)(2,1)} %copy-done.1, s32[]{:T(128)S(6)} %select_n.32, ...), kind=kLoop, calls=%fused_computation.23 | loop fusion | flops 884736 | bytes 1523860 | tf_op jit(solution)/shard_map/add | solution.py:463
  (7 shorter events, 0.0 us)
Async XLA Ops:
  0.0 126.9 %copy-start = (bf16[256,3072]{1,0:T(8,128)(2,1)S(1)}, bf16[256,3072]{1,0:T(8,128)(2,1)}, u32[]{:S(2)}) copy-start(bf16[256,3072]{1,0:T(8,128)(2,1)} %param.18) | copy-start | bytes 4718596
  4.0 1.0 copy-start.2
  4.9 0.9 copy-start.3
  5.9 0.9 copy-start.4
  89.7 23.6 %copy-start.1 = (bf16[384,3072]{1,0:T(8,128)(2,1)}, bf16[384,3072]{1,0:T(8,128)(2,1)S(1)}, u32[]{:S(2)}) copy-start(bf16[384,3072]{1,0:T(8,128)(2,1)S(1)} %get-tuple-element.8) | copy-start | bytes 7077892
  114.1 12.8 %copy-start.5 = (bf16[384,256]{1,0:T(8,128)(2,1)S(1)}, bf16[384,256]{1,0:T(8,128)(2,1)}, u32[]{:S(2)}) copy-start(bf16[384,256]{1,0:T(8,128)(2,1)} %attend.1) | copy-start | bytes 589828

commit v4 on v3

--- a/solution.py
+++ b/solution.py
@@ -1,3 +1,4 @@
+import functools
 import math
 
 import jax
@@ -173,7 +174,14 @@
 COPIES = 2 * (Z - 1) + 6 * Z + 2 * Y * Z + 9
 
 
-def gather_kernel(tokens, keys, values, whole, key_all, value_all, send, recv, local):
+LN_ROWS = 32
+
+
+def gather_kernel(
+    ends_ref, modulation, tokens, keys, values, w_in_hbm, w_out_hbm,
+    whole, key_all, value_all, part,
+    w_in, w_out, modulated, hidden, send, recv, local,
+):
     rows = keys.shape[0]
     me = lax.axis_index("ctx")
     y, z, core = me // (Z * CORES), me // CORES % Z, me % CORES
@@ -229,6 +237,11 @@
 
     stay = [pltpu.make_async_copy(own[w], slot(w, 0, 0), local.at[w]) for w in (0, 1)]
     stay.append(pltpu.make_async_copy(tokens, strip(0), local.at[2]))
+    weights = [
+        pltpu.make_async_copy(w_in_hbm, w_in, local.at[3]),
+        pltpu.make_async_copy(w_out_hbm, w_out, local.at[4]),
+    ]
+    stay += weights
     for copy in stay:
         copy.start()
     near = [[None] * 4 for _ in range(Z)]
@@ -272,6 +285,33 @@
             pass_on(strip(1, flip, 1), strip(1, flip, 1), left),
         ]
 
+    def normalize(first, last):
+        @pl.loop(first // LN_ROWS, last // LN_ROWS)
+        def _(block):
+            start = pl.multiple_of(block * LN_ROWS, LN_ROWS)
+            values = whole[pl.ds(start, LN_ROWS), :].astype(jnp.float32)
+            centred = values - jnp.mean(values, axis=1, keepdims=True)
+            variance = jnp.mean(centred * centred, axis=1, keepdims=True)
+            normed = centred * lax.rsqrt(variance + eps_norm)
+            pos = me * rows + start + lax.broadcasted_iota(jnp.int32, (LN_ROWS, 1), 0)
+            shift = jnp.broadcast_to(modulation[0, 0:1, :], normed.shape)
+            scale = jnp.broadcast_to(modulation[1, 0:1, :], normed.shape)
+            for clip in range(1, modulation.shape[1]):
+                later = pos >= ends_ref[clip - 1]
+                shift = jnp.where(later, modulation[0, clip:clip + 1, :], shift)
+                scale = jnp.where(later, modulation[1, clip:clip + 1, :], scale)
+            modulated[pl.ds(start, LN_ROWS), :] = (normed * (1.0 + scale) + shift).astype(
+                modulated.dtype
+            )
+
+    def project(source, weight, target, width, finish_tile):
+        @pl.loop(0, weight.shape[1] // width)
+        def _(block):
+            cols = pl.ds(pl.multiple_of(block * width, width), width)
+            target[:, cols] = finish_tile(
+                jnp.dot(source[...], weight[:, cols], preferred_element_type=jnp.float32)
+            ).astype(target.dtype)
+
     ends = tokens_far(sides, False)
     order = (0, 1, 3, 2)
     for i, dz in enumerate(order):
@@ -279,6 +319,8 @@
             for w in (0, 1):
                 to_z[dz][w].wait_recv()
             spread(dz)
+            if i == 3:
+                normalize(rows // 2, rows)
             relay(order[i - 1])
         if i == 1:
             over.wait_recv()
@@ -287,20 +329,26 @@
             ends += tokens_far(sides, True)
         if i > 1:
             finish(order[i - 2])
-    for copy in ends:
-        copy.wait_recv()
+        if i == 2:
+            for copy in ends:
+                copy.wait_recv()
+            for copy in stay:
+                copy.wait()
+            normalize(0, rows // 2)
+    project(
+        modulated, w_in, hidden, 256, functools.partial(jax.nn.gelu, approximate=True)
+    )
     relay(order[Z - 1])
+    project(hidden, w_out, part, 512, lambda tile: tile)
     finish(order[Z - 2])
     finish(order[Z - 1])
     for copy in to_core:
         copy.wait_recv()
     for copy in started:
         copy.wait_send()
-    for copy in stay:
-        copy.wait()
-
-
-def gather_rows(tokens, keys, values, devices, leads):
+
+
+def gather_rows(clip_end, modulation, tokens, keys, values, w_in, w_out, devices, leads):
     rows, width = keys.shape
     hbm = pl.BlockSpec(memory_space=pl.ANY)
     vmem = pl.BlockSpec(memory_space=pltpu.VMEM)
@@ -311,19 +359,24 @@
             jax.ShapeDtypeStruct((rows, tokens.shape[1] * leads), tokens.dtype),
             gathered,
             gathered,
+            jax.ShapeDtypeStruct((rows, w_out.shape[1]), jnp.float32),
         ),
-        in_specs=[hbm, hbm, hbm],
-        out_specs=(vmem, hbm, hbm),
+        in_specs=[pl.BlockSpec(memory_space=pltpu.SMEM), vmem, hbm, hbm, hbm, hbm, hbm],
+        out_specs=(vmem, hbm, hbm, vmem),
         scratch_shapes=[
+            pltpu.VMEM(w_in.shape, w_in.dtype),
+            pltpu.VMEM(w_out.shape, w_out.dtype),
+            pltpu.VMEM((rows, w_in.shape[0]), jnp.bfloat16),
+            pltpu.VMEM((rows, w_in.shape[1]), jnp.bfloat16),
             pltpu.SemaphoreType.DMA((COPIES,)),
             pltpu.SemaphoreType.DMA((COPIES,)),
-            pltpu.SemaphoreType.DMA((3,)),
+            pltpu.SemaphoreType.DMA((5,)),
         ],
         compiler_params=pltpu.CompilerParams(
-            collective_id=0, has_side_effects=True, vmem_limit_bytes=48 << 20
+            collective_id=0, has_side_effects=True, vmem_limit_bytes=60 << 20
         ),
         name="gather_all",
-    )(tokens, keys, values)
+    )(clip_end, modulation, tokens, keys, values, w_in, w_out)
 
 
 CHUNKS = 4
@@ -431,28 +484,14 @@
     tp_size = lax.axis_size("tp")
     clips = causal.shape[0]
     first_row = lax.axis_index("ctx") * local_rows
-    whole_rows, key_all, value_all = gather_rows(
-        tokens, key_rows, value_rows, lax.axis_size("ctx"), tp_size
-    )
     numbers = jnp.arange(clips, dtype=jnp.int32)
     clip_end = jnp.sum((clip_ids[None, :] <= numbers[:, None]).astype(jnp.int32), axis=1)
-    own_ids = clips_at(first_row + jnp.arange(local_rows, dtype=jnp.int32), clip_end)
-    token_values = whole_rows.astype(jnp.float32)
-    row_mean = jnp.mean(token_values, axis=1, keepdims=True)
-    centred = token_values - row_mean
-    row_var = jnp.mean(centred * centred, axis=1, keepdims=True)
-    normed = centred * lax.rsqrt(row_var + eps_norm)
-    shift_rows = pick_rows(own_ids, modulation[0])
-    scale_rows = pick_rows(own_ids, modulation[1])
-    modulated = (normed * (1.0 + scale_rows) + shift_rows).astype(jnp.bfloat16)
-    hidden = jax.nn.gelu(
-        jnp.dot(modulated, w_mlp, preferred_element_type=jnp.float32), approximate=True
-    ).astype(jnp.bfloat16)
-
+    whole_rows, key_all, value_all, mlp_part = gather_rows(
+        clip_end, modulation, tokens, key_rows, value_rows, w_mlp, w_mlp_out,
+        lax.axis_size("ctx"), tp_size,
+    )
     attended = attention(queries, key_all, value_all, jnp.concatenate([clip_end, causal]))
-    part = jnp.dot(attended, w_attn_out, preferred_element_type=jnp.float32) + jnp.dot(
-        hidden, w_mlp_out, preferred_element_type=jnp.float32
-    )
+    part = jnp.dot(attended, w_attn_out, preferred_element_type=jnp.float32) + mlp_part
     branch = reduce_rows(part.astype(jnp.bfloat16))
     share_rows = local_rows // tp_size
     first_share = lax.axis_index("tp") * share_rows

time: 178 us -> 164 us (0.921)
  matrix products: 15.9 us -> 3.24 us
  Pallas kernels: 151 us -> 155 us
  local copies, waits for them, and re-layouts: 4.14 us -> 1.01 us
    dot_general x2 -> x1, matrix products: 15.9 us -> 3.24 us  [per_device(): jnp.dot(attended, w_attn_out, preferred_element_type=jnp.float32) + mlp_part]
    pallas_call x1, Pallas kernels: 82.9 us -> 87 us  [gather_rows(): pl.pallas_call(gather_kernel, out_shape=(jax.ShapeDtypeStruct((rows, toke...]
    unnamed x12 -> x6, local copies, waits for them, and re-layouts: 2.82 us -> 0.01 us
where the time goes in v4:
time: 164 us; the launch traced here: 163 us
  Pallas kernels  155 us (95%)
  other arithmetic  4.38 us (3%)
  matrix products  3.24 us (2%)
    pallas_call x1, Pallas kernels, gather_rows(): pl.pallas_call(gather_kernel, out_shape=(jax.ShapeDtypeStruct((rows, toke...  87 us
    pallas_call x1, Pallas kernels, reduce_rows(): pl.pallas_call(reduce_kernel, out_shape=jax.ShapeDtypeStruct((rows, width...  44.3 us
    pallas_call x1, Pallas kernels, attention(): pl.pallas_call(attend_kernel, out_shape=jax.ShapeDtypeStruct((rows, width...  23.2 us

profile of v4, /device:TPU:112, one launch (start us, length us, event | category | flops | bytes accessed | tf_op | source)
XLA Modules:
  0.0 163.2 jit_solution(5574312102677402040)
XLA Ops:
  0.0 0.0 copy-start
  0.0 1.6 %convert_reduce_fusion.ends_ref = s32[4]{0:T(128)} fusion(s32[12288]{0:T(1024)} %param.14), kind=kLoop, calls=%fused_computation.2 | loop fusion | flops 147452 | bytes 49168 | tf_op jit(solution)/shard_map/reduce_sum | solution.py:488
  1.6 0.0 copy-start.1
  1.6 0.0 copy-start.2
  1.6 87.0 %gather_all.1 = (bf16[384,3072]{1,0:T(8,128)(2,1)}, bf16[12288,256]{1,0:T(8,128)(2,1)}, bf16[12288,256]{1,0:T(8,128)(2,1)}, f32[384,3072]{1,0:T(8,128)}) custom-call(s32[4]{0:T(128)} %convert_reduce_fusion.ends_ref, f32[3,4,3072]{2,1,0:T(4,128)} %modulation.1, bf16[384,384]{1,0:T(8,128)(2,1)} %tokens.1, bf16[384,256]{1,0:T(8,128)(2,1)} %keys.1, ...), custom_call_target="tpu_custom_call" | custom-call | tf_op jit(solution)/shard_map/gather_all/pallas_call | solution.py:356
  88.7 0.0 copy-done.1
  88.7 0.0 copy-done.2
  88.7 0.6 pad_add_fusion.table
  89.4 23.2 %attend.1 = bf16[384,256]{1,0:T(8,128)(2,1)} custom-call(s32[8]{0:T(128)} %pad_add_fusion.table, bf16[384,256]{1,0:T(8,128)(2,1)} %q_ref.1, bf16[12288,256]{1,0:T(8,128)(2,1)} %get-tuple-element.10.k_ref, bf16[12288,256]{1,0:T(8,128)(2,1)} %get-tuple-element.11.v_ref), custom_call_target="tpu_custom_call" | custom-call | flops 9663676416 | bytes 12582912 | tf_op jit(solution)/shard_map/attend/pallas_call | solution.py:128
  112.6 0.0 copy-done
  112.6 3.2 %add_convert_fusion.part = bf16[384,3072]{1,0:T(8,128)(2,1)S(1)} fusion(f32[384,3072]{1,0:T(8,128)} %get-tuple-element.12, bf16[384,256]{1,0:T(8,128)(2,1)} %attend.1, bf16[256,3072]{1,0:T(8,128)(2,1)S(1)} %copy-done), kind=kOutput, calls=%fused_computation | convolution fusion | flops 606339072 | bytes 8847360 | tf_op jit(solution)/shard_map/dot_general | solution.py:494
  115.8 44.3 %reduce_branch.1 = f32[48,3072]{1,0:T(8,128)S(1)} custom-call(bf16[384,3072]{1,0:T(8,128)(2,1)S(1)} %add_convert_fusion.part), custom_call_target="tpu_custom_call" | custom-call | bytes 100000000 | tf_op jit(solution)/shard_map/reduce_branch/pallas_call | solution.py:458
  160.1 0.1 convert_reduce_fusion.1
  160.2 1.0 fusion
  161.2 2.0 %multiply_add_fusion = f32[48,3072]{1,0:T(8,128)} fusion(f32[48,3072]{1,0:T(8,128)S(1)} %reduce_branch.1, f32[3072]{0:T(1024)S(1)} %bitcast.9, f32[3072]{0:T(1024)S(1)} %bitcast.10, f32[3072]{0:T(1024)S(1)} %bitcast.8, f32[3072]{0:T(1024)S(1)} %bitcast.7, bf16[384,3072]{1,0:T(8,128)(2,1)} %get-tuple-element.9, s32[]{:T(128)S(6)} %select_n.13, ...), kind=kLoop, calls=%fused_computation.1 | loop fusion | flops 884736 | bytes 1523860 | tf_op jit(solution)/shard_map/add | solution.py:502
  (2 shorter events, 0.0 us)
Async XLA Ops:
  0.0 112.6 %copy-start = (bf16[256,3072]{1,0:T(8,128)(2,1)S(1)}, bf16[256,3072]{1,0:T(8,128)(2,1)}, u32[]{:S(2)}) copy-start(bf16[256,3072]{1,0:T(8,128)(2,1)} %param.18) | copy-start | bytes 4718596
  1.6 87.1 %copy-start.1 = (s32[4]{0:T(128)S(1)}, s32[4]{0:T(128)}, u32[]{:S(2)}) copy-start(s32[4]{0:T(128)} %convert_reduce_fusion.ends_ref) | copy-start | bytes 52
  1.6 87.1 %copy-start.2 = (s32[4]{0:T(128)S(1)}, s32[4]{0:T(128)}, u32[]{:S(2)}) copy-start(s32[4]{0:T(128)} %param.15) | copy-start | bytes 52

commit v5 on v4

--- a/solution.py
+++ b/solution.py
@@ -14,13 +14,6 @@
 eps_norm = 1e-06
 
 
-def pick_rows(clip_rows, table):
-    out = jnp.broadcast_to(table[0][None, :], (clip_rows.shape[0], table.shape[1]))
-    for clip in range(1, table.shape[0]):
-        out = jnp.where(clip_rows[:, None] == clip, table[clip][None, :], out)
-    return out
-
-
 def interval(table, first, rows):
     clips = table.shape[0] // 2
 
@@ -37,10 +30,6 @@
     end = jnp.where(table[clips + high] == 0, table[high], first + rows)
     whole_end = jnp.where(table[clips + low] == 0, table[low], first + 1)
     return start_of(low), end, start_of(high), whole_end
-
-
-def clips_at(positions, clip_end):
-    return jnp.sum((positions[:, None] >= clip_end[None, :-1]).astype(jnp.int32), axis=1)
 
 
 def attend_kernel(table, q_ref, k_ref, v_ref, out_ref, acc, peak, edges):
@@ -171,7 +160,7 @@
 
 Y, Z, CORES = 4, 4, 2
 X, HI = 4, 2
-COPIES = 2 * (Z - 1) + 6 * Z + 2 * Y * Z + 9
+COPIES = 2 * (Z - 1) + 6 * Z + 2 * Y * Z + 12
 
 
 LN_ROWS = 32
@@ -180,7 +169,7 @@
 def gather_kernel(
     ends_ref, modulation, tokens, keys, values, w_in_hbm, w_out_hbm,
     whole, key_all, value_all, part,
-    w_in, w_out, modulated, hidden, send, recv, local,
+    w_in, w_out, modulated, hidden, halfway, send, recv, local,
 ):
     rows = keys.shape[0]
     me = lax.axis_index("ctx")
@@ -213,11 +202,22 @@
         return whole.at[pl.ds(part * half, half), cols]
 
     right, left = {"tp": column(1)}, {"tp": column(-1)}
-    across = {"tp": column(0, True)}
+    depth = hi * Z + z
+
+    def along(steps):
+        place = (depth + steps + Z * HI) % (Z * HI)
+        return {"ctx": (y * Z + place % Z) * CORES + core, "tp": x * HI + place // Z}
+
+    up, down = along(2), along(-2)
     greet(
         [at(0, d) for d in range(1, Z)]
-        + [at(1, 0), at(-1, 0), at(0, 0, True), right, left, across]
+        + [at(1, 0), at(-1, 0), at(0, 0, True), right, left, up, down]
     )
+
+    def origin(steps, part):
+        lead_there = along(steps)["tp"]
+        cols = pl.ds(pl.multiple_of(lead_there * wide, wide), wide)
+        return whole.at[pl.ds(part * half, half), cols]
     started = []
     made = [0]
 
@@ -229,7 +229,10 @@
         started.append(copy)
         return copy
 
-    over = pass_on(tokens, strip(0), across)
+    over = [
+        pass_on(tokens.at[pl.ds(0, half)], halfway.at[0], up),
+        pass_on(tokens.at[pl.ds(half, half)], halfway.at[1], down),
+    ]
     sides = [pass_on(tokens, strip(0), right), pass_on(tokens, strip(0), left)]
 
     def make(src, which, owner, target):
@@ -313,6 +316,12 @@
             ).astype(target.dtype)
 
     ends = tokens_far(sides, False)
+    for copy in over:
+        copy.wait_recv()
+    over = [
+        pass_on(halfway.at[0], origin(-2, 0), up),
+        pass_on(halfway.at[1], origin(2, 1), down),
+    ]
     order = (0, 1, 3, 2)
     for i, dz in enumerate(order):
         if i > 0:
@@ -323,7 +332,8 @@
                 normalize(rows // 2, rows)
             relay(order[i - 1])
         if i == 1:
-            over.wait_recv()
+            for copy in over:
+                copy.wait_recv()
             sides = [pass_on(strip(0, True), strip(0, True), to) for to in (right, left)]
         if i == 2:
             ends += tokens_far(sides, True)
@@ -368,6 +378,7 @@
             pltpu.VMEM(w_out.shape, w_out.dtype),
             pltpu.VMEM((rows, w_in.shape[0]), jnp.bfloat16),
             pltpu.VMEM((rows, w_in.shape[1]), jnp.bfloat16),
+            pltpu.VMEM((2, rows // 2, tokens.shape[1]), tokens.dtype),
             pltpu.SemaphoreType.DMA((COPIES,)),
             pltpu.SemaphoreType.DMA((COPIES,)),
             pltpu.SemaphoreType.DMA((5,)),
@@ -382,7 +393,10 @@
 CHUNKS = 4
 
 
-def reduce_kernel(part, out, held, relayed, outgoing, incoming, sums, send, recv):
+def reduce_kernel(
+    ends_ref, modulation, whole, part,
+    out, held, relayed, outgoing, incoming, sums, residual, send, recv, local,
+):
     rows = part.shape[0] // (X * HI)
     wide = part.shape[1] // CHUNKS
     me = lax.axis_index("tp")
@@ -391,6 +405,9 @@
     left = {"tp": (x + X - 1) % X * HI + hi}
     across = {"tp": x * HI + 1 - hi}
     greet([left, right, across])
+    mine = pl.ds(pl.multiple_of(me * rows, rows), rows)
+    fetch = pltpu.make_async_copy(whole.at[mine], residual, local)
+    fetch.start()
 
     def piece(dx, first, count, chunk):
         start = pl.multiple_of(((x + dx) % X * HI + first) * rows, rows)
@@ -443,22 +460,32 @@
         if c > 0:
             combine(c - 1)
     combine(CHUNKS - 1)
+    fetch.wait()
+    first = (lax.axis_index("ctx") * X * HI + me) * rows
+    pos = first + lax.broadcasted_iota(jnp.int32, (rows, 1), 0)
     for c in range(CHUNKS):
         copies[c][6].wait_recv()
-        out[:, cols(c)] = sums[c] + incoming[c].astype(jnp.float32)
+        branch = sums[c] + incoming[c].astype(jnp.float32)
+        gate = jnp.broadcast_to(modulation[2, 0:1, cols(c)], branch.shape)
+        for clip in range(1, modulation.shape[1]):
+            later = pos >= ends_ref[clip - 1]
+            gate = jnp.where(later, modulation[2, clip:clip + 1, cols(c)], gate)
+        out[:, cols(c)] = residual[:, cols(c)].astype(jnp.float32) + gate * branch
     for mine in copies:
         for made in mine:
             made.wait_send()
 
 
-def reduce_rows(part):
+def reduce_rows(clip_end, modulation, whole, part):
     rows, width = part.shape[0] // (X * HI), part.shape[1]
     wide = width // CHUNKS
     vmem = pl.BlockSpec(memory_space=pltpu.VMEM)
     return pl.pallas_call(
         reduce_kernel,
         out_shape=jax.ShapeDtypeStruct((rows, width), jnp.float32),
-        in_specs=[vmem],
+        in_specs=[
+            pl.BlockSpec(memory_space=pltpu.SMEM), vmem, pl.BlockSpec(memory_space=pl.ANY), vmem
+        ],
         out_specs=vmem,
         scratch_shapes=[
             pltpu.VMEM((3, CHUNKS, HI * rows, wide), jnp.bfloat16),
@@ -466,15 +493,17 @@
             pltpu.VMEM((CHUNKS, rows, wide), jnp.bfloat16),
             pltpu.VMEM((CHUNKS, rows, wide), jnp.bfloat16),
             pltpu.VMEM((CHUNKS, rows, wide), jnp.float32),
+            pltpu.VMEM((rows, width), jnp.bfloat16),
             pltpu.SemaphoreType.DMA((CHUNKS, 7)),
             pltpu.SemaphoreType.DMA((CHUNKS, 7)),
+            pltpu.SemaphoreType.DMA,
         ],
         compiler_params=pltpu.CompilerParams(
             collective_id=1, has_side_effects=True, vmem_limit_bytes=24 << 20
         ),
         cost_estimate=pl.CostEstimate(flops=0, bytes_accessed=100_000_000, transcendentals=0),
         name="reduce_branch",
-    )(part)
+    )(clip_end, modulation, whole, part)
 
 
 def per_device(
@@ -483,7 +512,6 @@
     local_rows = queries.shape[0]
     tp_size = lax.axis_size("tp")
     clips = causal.shape[0]
-    first_row = lax.axis_index("ctx") * local_rows
     numbers = jnp.arange(clips, dtype=jnp.int32)
     clip_end = jnp.sum((clip_ids[None, :] <= numbers[:, None]).astype(jnp.int32), axis=1)
     whole_rows, key_all, value_all, mlp_part = gather_rows(
@@ -492,14 +520,7 @@
     )
     attended = attention(queries, key_all, value_all, jnp.concatenate([clip_end, causal]))
     part = jnp.dot(attended, w_attn_out, preferred_element_type=jnp.float32) + mlp_part
-    branch = reduce_rows(part.astype(jnp.bfloat16))
-    share_rows = local_rows // tp_size
-    first_share = lax.axis_index("tp") * share_rows
-    share_ids = clips_at(
-        first_row + first_share + jnp.arange(share_rows, dtype=jnp.int32), clip_end
-    )
-    residual = lax.dynamic_slice_in_dim(whole_rows, first_share, share_rows, 0).astype(jnp.float32)
-    return residual + pick_rows(share_ids, modulation[2]) * branch
+    return reduce_rows(clip_end, modulation, whole_rows, part.astype(jnp.bfloat16))
 
 
 def solution(mesh):

time: 164 us -> 161 us (0.982)
  other arithmetic: 4.38 us -> 2.36 us
  Pallas kernels: 155 us -> 153 us
    pallas_call x1, Pallas kernels: 87 us -> 92.6 us  [gather_rows(): pl.pallas_call(gather_kernel, out_shape=(jax.ShapeDtypeStruct((rows, toke...]
    pallas_call x1, Pallas kernels: 44.3 us -> 39.3 us  [reduce_rows(): pl.pallas_call(reduce_kernel, out_shape=jax.ShapeDtypeStruct((rows, width...]
    add x2 -> x0, other arithmetic: 1.99 us -> none  [the longest x1 1.99 us: per_device(): return residual + pick_rows(share_ids, modulation[2]) * branch]
    pallas_call x1, Pallas kernels: 23.2 us -> 21.3 us  [attention(): pl.pallas_call(attend_kernel, out_shape=jax.ShapeDtypeStruct((rows, width...]
where the time goes in v5:
time: 161 us; the launch traced here: 160 us
  Pallas kernels  153 us (95%)
  matrix products  3.37 us (2%)
  other arithmetic  2.36 us (1%)
    pallas_call x1, Pallas kernels, gather_rows(): pl.pallas_call(gather_kernel, out_shape=(jax.ShapeDtypeStruct((rows, toke...  92.6 us
    pallas_call x1, Pallas kernels, reduce_rows(): pl.pallas_call(reduce_kernel, out_shape=jax.ShapeDtypeStruct((rows, width...  39.3 us
    pallas_call x1, Pallas kernels, attention(): pl.pallas_call(attend_kernel, out_shape=jax.ShapeDtypeStruct((rows, width...  21.3 us
    dot_general x1, matrix products, per_device(): jnp.dot(attended, w_attn_out, preferred_element_type=jnp.float32) + mlp_part  3.37 us

profile of v5, /device:TPU:112, one launch (start us, length us, event | category | flops | bytes accessed | tf_op | source)
XLA Modules:
  0.0 159.9 jit_solution(3963785939094640208)
XLA Ops:
  0.0 0.0 copy-start
  0.0 1.1 convert_reduce_fusion.ends_ref
  1.1 0.0 copy-start.3
  1.1 1.2 pad_add_fusion.table
  2.4 0.0 copy-done.3
  2.4 92.6 %gather_all.1 = (bf16[384,3072]{1,0:T(8,128)(2,1)}, bf16[12288,256]{1,0:T(8,128)(2,1)}, bf16[12288,256]{1,0:T(8,128)(2,1)}, f32[384,3072]{1,0:T(8,128)}) custom-call(s32[4]{0:T(128)} %copy-done.3, f32[3,4,3072]{2,1,0:T(4,128)} %modulation.3, bf16[384,384]{1,0:T(8,128)(2,1)} %tokens.1, bf16[384,256]{1,0:T(8,128)(2,1)} %keys.1, bf16[384,256]{1,0:T(8,128)(2,1)} %values.1, ...), custom_call_target="tpu_custom_call" | custom-call | tf_op jit(solution)/shard_map/gather_all/pallas_call | solution.py:366
  95.0 21.3 %attend.1 = bf16[384,256]{1,0:T(8,128)(2,1)} custom-call(s32[8]{0:T(128)} %pad_add_fusion.table, bf16[384,256]{1,0:T(8,128)(2,1)} %q_ref.1, bf16[12288,256]{1,0:T(8,128)(2,1)} %get-tuple-element.10.k_ref, bf16[12288,256]{1,0:T(8,128)(2,1)} %get-tuple-element.11.v_ref), custom_call_target="tpu_custom_call" | custom-call | flops 9663676416 | bytes 12582912 | tf_op jit(solution)/shard_map/attend/pallas_call | solution.py:117
  116.3 0.0 copy-done
  116.3 0.0 copy-start.1
  116.3 0.0 copy-start.2
  116.3 0.0 copy-start.4
  116.3 3.4 %add_convert_fusion.part = bf16[384,3072]{1,0:T(8,128)(2,1)S(1)} fusion(f32[384,3072]{1,0:T(8,128)} %get-tuple-element.12, bf16[384,256]{1,0:T(8,128)(2,1)} %attend.1, bf16[256,3072]{1,0:T(8,128)(2,1)S(1)} %copy-done), kind=kOutput, calls=%fused_computation | convolution fusion | flops 606339072 | bytes 8847360 | tf_op jit(solution)/shard_map/dot_general | solution.py:522
  119.7 0.0 copy-done.1
  119.7 0.0 copy-done.2
  119.7 0.0 copy-done.4
  119.7 39.3 %reduce_branch.1 = f32[48,3072]{1,0:T(8,128)S(1)} custom-call(s32[4]{0:T(128)S(1)} %copy-done.4, f32[3,4,3072]{2,1,0:T(4,128)S(1)} %copy-done.2, bf16[384,3072]{1,0:T(8,128)(2,1)S(1)} %copy-done.1, bf16[384,3072]{1,0:T(8,128)(2,1)S(1)} %add_convert_fusion.part), custom_call_target="tpu_custom_call" | custom-call | bytes 100000000 | tf_op jit(solution)/shard_map/reduce_branch/pallas_call | solution.py:483
  159.1 0.8 copy.12
Async XLA Ops:
  0.0 116.3 %copy-start = (bf16[256,3072]{1,0:T(8,128)(2,1)S(1)}, bf16[256,3072]{1,0:T(8,128)(2,1)}, u32[]{:S(2)}) copy-start(bf16[256,3072]{1,0:T(8,128)(2,1)} %param.18) | copy-start | bytes 4718596
  1.1 1.2 copy-start.3
  116.3 3.4 %copy-start.1 = (bf16[384,3072]{1,0:T(8,128)(2,1)S(1)}, bf16[384,3072]{1,0:T(8,128)(2,1)}, u32[]{:S(2)}) copy-start(bf16[384,3072]{1,0:T(8,128)(2,1)} %get-tuple-element.9.whole) | copy-start | bytes 7077892
  116.3 3.4 %copy-start.2 = (f32[3,4,3072]{2,1,0:T(4,128)S(1)}, f32[3,4,3072]{2,1,0:T(4,128)}, u32[]{:S(2)}) copy-start(f32[3,4,3072]{2,1,0:T(4,128)} %modulation.3) | copy-start | bytes 442372
  116.3 3.4 %copy-start.4 = (s32[4]{0:T(128)S(1)}, s32[4]{0:T(128)}, u32[]{:S(2)}) copy-start(s32[4]{0:T(128)} %copy-done.3) | copy-start | bytes 52

commit v6 on v5

--- a/solution.py
+++ b/solution.py
@@ -169,7 +169,7 @@
 def gather_kernel(
     ends_ref, modulation, tokens, keys, values, w_in_hbm, w_out_hbm,
     whole, key_all, value_all, part,
-    w_in, w_out, modulated, hidden, halfway, send, recv, local,
+    w_in, w_out, modulated, hidden, halfway, stage, send, recv, local,
 ):
     rows = keys.shape[0]
     me = lax.axis_index("ctx")
@@ -188,6 +188,8 @@
     def at(dy, dz, flip=False):
         return {"ctx": index(dy, dz, flip)}
 
+    apart = (0, 1 - 2 * (z % 2), 2 - 4 * (z // 2), 3 - 2 * z)
+
     lead = lax.axis_index("tp")
     x, hi = lead // HI, lead % HI
     half, wide = tokens.shape[0] // 2, tokens.shape[1]
@@ -210,7 +212,7 @@
 
     up, down = along(2), along(-2)
     greet(
-        [at(0, d) for d in range(1, Z)]
+        [at(0, apart[r]) for r in range(1, Z)]
         + [at(1, 0), at(-1, 0), at(0, 0, True), right, left, up, down]
     )
 
@@ -229,60 +231,66 @@
         started.append(copy)
         return copy
 
-    over = [
-        pass_on(tokens.at[pl.ds(0, half)], halfway.at[0], up),
-        pass_on(tokens.at[pl.ds(half, half)], halfway.at[1], down),
-    ]
+    def swap(r):
+        return [
+            pass_on(own[w], slot(w, 0, 0), at(0, apart[r])) for w in (0, 1)
+        ]
+
+    to_z = [None, swap(1), None, None]
     sides = [pass_on(tokens, strip(0), right), pass_on(tokens, strip(0), left)]
 
     def make(src, which, owner, target):
         return pass_on(src, slot(which, *owner), at(*target))
 
-    stay = [pltpu.make_async_copy(own[w], slot(w, 0, 0), local.at[w]) for w in (0, 1)]
-    stay.append(pltpu.make_async_copy(tokens, strip(0), local.at[2]))
+    enter = [pltpu.make_async_copy(own[w], stage.at[w], local.at[w]) for w in (0, 1)]
+    leave = [
+        pltpu.make_async_copy(stage.at[w], slot(w, 0, 0), local.at[5 + w]) for w in (0, 1)
+    ]
+    stay = [pltpu.make_async_copy(tokens, strip(0), local.at[2])]
     weights = [
         pltpu.make_async_copy(w_in_hbm, w_in, local.at[3]),
         pltpu.make_async_copy(w_out_hbm, w_out, local.at[4]),
     ]
     stay += weights
-    for copy in stay:
+    for copy in enter + stay:
         copy.start()
     near = [[None] * 4 for _ in range(Z)]
     far = [[None] * 2 for _ in range(Z)]
-    to_z = [[None] * 2 for _ in range(Z)]
     to_core = []
 
-    def spread(dz):
+    def spread(r):
+        dz = apart[r]
         for w in (0, 1):
-            src = own[w] if dz == 0 else slot(w, 0, dz)
-            near[dz][w] = make(src, w, (0, dz), (1, 0))
-            near[dz][2 + w] = make(src, w, (0, dz), (-1, 0))
+            src = own[w] if r == 0 else slot(w, 0, dz)
+            near[r][w] = make(src, w, (0, dz), (1, 0))
+            near[r][2 + w] = make(src, w, (0, dz), (-1, 0))
             to_core.append(make(src, w, (0, dz), (0, 0, True)))
 
-    def relay(dz):
-        near[dz][0].wait_recv()
-        far[dz][0] = make(slot(0, -1, dz), 0, (-1, dz), (1, 0))
-        near[dz][3].wait_recv()
-        far[dz][1] = make(slot(1, 1, dz), 1, (1, dz), (-1, 0))
-        near[dz][1].wait_recv()
-        near[dz][2].wait_recv()
+    def relay(r):
+        dz = apart[r]
+        near[r][0].wait_recv()
+        far[r][0] = make(slot(0, -1, dz), 0, (-1, dz), (1, 0))
+        near[r][3].wait_recv()
+        far[r][1] = make(slot(1, 1, dz), 1, (1, dz), (-1, 0))
+        near[r][1].wait_recv()
+        near[r][2].wait_recv()
         for w in (0, 1):
             for dy in (-1, 1):
                 to_core.append(make(slot(w, dy, dz), w, (dy, dz), (0, 0, True)))
 
-    def finish(dz):
+    def finish(r):
         for w in (0, 1):
-            far[dz][w].wait_recv()
-            to_core.append(make(slot(w, 2, dz), w, (2, dz), (0, 0, True)))
-
-    for d in (1, 3, 2):
-        for w in (0, 1):
-            to_z[Z - d][w] = make(own[w], w, (0, 0), (0, d))
+            far[r][w].wait_recv()
+            to_core.append(make(slot(w, 2, apart[r]), w, (2, apart[r]), (0, 0, True)))
+
+    def arrived(copies):
+        for copy in copies:
+            copy.wait_recv()
+
     spread(0)
 
-    def tokens_far(arrived, flip):
-        for copy in arrived:
-            copy.wait_recv()
+    def tokens_far(copies, flip):
+        arrived(copies)
         return [
             pass_on(strip(-1, flip, 0), strip(-1, flip, 0), right),
             pass_on(strip(1, flip, 1), strip(1, flip, 1), left),
@@ -315,43 +323,49 @@
                 jnp.dot(source[...], weight[:, cols], preferred_element_type=jnp.float32)
             ).astype(target.dtype)
 
+    arrived(to_z[1])
+    to_z[2] = swap(2)
+    spread(1)
+    over = [
+        pass_on(tokens.at[pl.ds(0, half)], halfway.at[0], up),
+        pass_on(tokens.at[pl.ds(half, half)], halfway.at[1], down),
+    ]
+    for copy in enter:
+        copy.wait()
+    for copy in leave:
+        copy.start()
     ends = tokens_far(sides, False)
-    for copy in over:
-        copy.wait_recv()
+    relay(0)
+    arrived(over)
     over = [
         pass_on(halfway.at[0], origin(-2, 0), up),
         pass_on(halfway.at[1], origin(2, 1), down),
     ]
-    order = (0, 1, 3, 2)
-    for i, dz in enumerate(order):
-        if i > 0:
-            for w in (0, 1):
-                to_z[dz][w].wait_recv()
-            spread(dz)
-            if i == 3:
-                normalize(rows // 2, rows)
-            relay(order[i - 1])
-        if i == 1:
-            for copy in over:
-                copy.wait_recv()
-            sides = [pass_on(strip(0, True), strip(0, True), to) for to in (right, left)]
-        if i == 2:
-            ends += tokens_far(sides, True)
-        if i > 1:
-            finish(order[i - 2])
-        if i == 2:
-            for copy in ends:
-                copy.wait_recv()
-            for copy in stay:
-                copy.wait()
-            normalize(0, rows // 2)
+    arrived(to_z[2])
+    to_z[3] = swap(3)
+    spread(2)
+    relay(1)
+    finish(0)
+    arrived(over)
+    sides = [pass_on(strip(0, True), strip(0, True), to) for to in (right, left)]
+    arrived(to_z[3])
+    spread(3)
+    ends += tokens_far(sides, True)
+    relay(2)
+    finish(1)
+    arrived(ends)
+    for copy in stay:
+        copy.wait()
+    normalize(0, rows)
+    relay(3)
+    finish(2)
     project(
         modulated, w_in, hidden, 256, functools.partial(jax.nn.gelu, approximate=True)
     )
-    relay(order[Z - 1])
+    finish(3)
     project(hidden, w_out, part, 512, lambda tile: tile)
-    finish(order[Z - 2])
-    finish(order[Z - 1])
+    for copy in leave:
+        copy.wait()
     for copy in to_core:
         copy.wait_recv()
     for copy in started:
@@ -379,9 +393,10 @@
             pltpu.VMEM((rows, w_in.shape[0]), jnp.bfloat16),
             pltpu.VMEM((rows, w_in.shape[1]), jnp.bfloat16),
             pltpu.VMEM((2, rows // 2, tokens.shape[1]), tokens.dtype),
+            pltpu.VMEM((2,) + keys.shape, keys.dtype),
             pltpu.SemaphoreType.DMA((COPIES,)),
             pltpu.SemaphoreType.DMA((COPIES,)),
-            pltpu.SemaphoreType.DMA((5,)),
+            pltpu.SemaphoreType.DMA((7,)),
         ],
         compiler_params=pltpu.CompilerParams(
             collective_id=0, has_side_effects=True, vmem_limit_bytes=60 << 20

time: 161 us -> 157 us (0.975)
  the two profiles are of different devices: /device:TPU:112 before, /device:TPU:40 now
where the time goes in v6:
time: 157 us
  Pallas kernels  150 us (96%)
  matrix products  3.37 us (2%)
  other arithmetic  2.36 us (2%)
    pallas_call x1, Pallas kernels, gather_rows(): pl.pallas_call(gather_kernel, out_shape=(jax.ShapeDtypeStruct((rows, toke...  90.5 us
    pallas_call x1, Pallas kernels, reduce_rows(): pl.pallas_call(reduce_kernel, out_shape=jax.ShapeDtypeStruct((rows, width...  38.3 us
    pallas_call x1, Pallas kernels, attention(): pl.pallas_call(attend_kernel, out_shape=jax.ShapeDtypeStruct((rows, width...  21.1 us
    dot_general x1, matrix products, per_device(): jnp.dot(attended, w_attn_out, preferred_element_type=jnp.float32) + mlp_part  3.37 us

profile of v6, /device:TPU:40, one launch (start us, length us, event | category | flops | bytes accessed | tf_op | source)
XLA Modules:
  0.0 156.6 jit_solution(2957806726583221196)
XLA Ops:
  0.0 0.0 copy-start
  0.0 1.1 convert_reduce_fusion.ends_ref
  1.1 0.0 copy-start.3
  1.1 1.2 pad_add_fusion.table
  2.4 0.0 copy-done.3
  2.4 90.5 %gather_all.1 = (bf16[384,3072]{1,0:T(8,128)(2,1)}, bf16[12288,256]{1,0:T(8,128)(2,1)}, bf16[12288,256]{1,0:T(8,128)(2,1)}, f32[384,3072]{1,0:T(8,128)}) custom-call(s32[4]{0:T(128)} %copy-done.3, f32[3,4,3072]{2,1,0:T(4,128)} %modulation.3, bf16[384,384]{1,0:T(8,128)(2,1)} %tokens.1, bf16[384,256]{1,0:T(8,128)(2,1)} %keys.1, bf16[384,256]{1,0:T(8,128)(2,1)} %values.1, ...), custom_call_target="tpu_custom_call" | custom-call | tf_op jit(solution)/shard_map/gather_all/pallas_call | solution.py:380
  92.9 21.1 %attend.1 = bf16[384,256]{1,0:T(8,128)(2,1)} custom-call(s32[8]{0:T(128)} %pad_add_fusion.table, bf16[384,256]{1,0:T(8,128)(2,1)} %q_ref.1, bf16[12288,256]{1,0:T(8,128)(2,1)} %get-tuple-element.10.k_ref, bf16[12288,256]{1,0:T(8,128)(2,1)} %get-tuple-element.11.v_ref), custom_call_target="tpu_custom_call" | custom-call | flops 9663676416 | bytes 12582912 | tf_op jit(solution)/shard_map/attend/pallas_call | solution.py:117
  114.0 0.0 copy-done
  114.0 0.0 copy-start.1
  114.0 0.0 copy-start.2
  114.0 0.0 copy-start.4
  114.0 3.4 %add_convert_fusion.part = bf16[384,3072]{1,0:T(8,128)(2,1)S(1)} fusion(f32[384,3072]{1,0:T(8,128)} %get-tuple-element.12, bf16[384,256]{1,0:T(8,128)(2,1)} %attend.1, bf16[256,3072]{1,0:T(8,128)(2,1)S(1)} %copy-done), kind=kOutput, calls=%fused_computation | convolution fusion | flops 606339072 | bytes 8847360 | tf_op jit(solution)/shard_map/dot_general | solution.py:537
  117.4 0.0 copy-done.1
  117.4 0.0 copy-done.2
  117.4 0.0 copy-done.4
  117.4 38.3 %reduce_branch.1 = f32[48,3072]{1,0:T(8,128)S(1)} custom-call(s32[4]{0:T(128)S(1)} %copy-done.4, f32[3,4,3072]{2,1,0:T(4,128)S(1)} %copy-done.2, bf16[384,3072]{1,0:T(8,128)(2,1)S(1)} %copy-done.1, bf16[384,3072]{1,0:T(8,128)(2,1)S(1)} %add_convert_fusion.part), custom_call_target="tpu_custom_call" | custom-call | bytes 100000000 | tf_op jit(solution)/shard_map/reduce_branch/pallas_call | solution.py:498
  155.7 0.8 copy.12
Async XLA Ops:
  0.0 114.0 %copy-start = (bf16[256,3072]{1,0:T(8,128)(2,1)S(1)}, bf16[256,3072]{1,0:T(8,128)(2,1)}, u32[]{:S(2)}) copy-start(bf16[256,3072]{1,0:T(8,128)(2,1)} %param.18) | copy-start | bytes 4718596
  1.1 1.2 copy-start.3
  114.0 3.4 %copy-start.1 = (bf16[384,3072]{1,0:T(8,128)(2,1)S(1)}, bf16[384,3072]{1,0:T(8,128)(2,1)}, u32[]{:S(2)}) copy-start(bf16[384,3072]{1,0:T(8,128)(2,1)} %get-tuple-element.9.whole) | copy-start | bytes 7077892
  114.0 3.4 %copy-start.2 = (f32[3,4,3072]{2,1,0:T(4,128)S(1)}, f32[3,4,3072]{2,1,0:T(4,128)}, u32[]{:S(2)}) copy-start(f32[3,4,3072]{2,1,0:T(4,128)} %modulation.3) | copy-start | bytes 442372
  114.0 3.4 %copy-start.4 = (s32[4]{0:T(128)S(1)}, s32[4]{0:T(128)}, u32[]{:S(2)}) copy-start(s32[4]{0:T(128)} %copy-done.3) | copy-start | bytes 52

commit v7 on v6

--- a/solution.py
+++ b/solution.py
@@ -237,6 +237,10 @@
         ]
 
     to_z = [None, swap(1), None, None]
+    over = [
+        pass_on(tokens.at[pl.ds(0, half)], halfway.at[0], up),
+        pass_on(tokens.at[pl.ds(half, half)], halfway.at[1], down),
+    ]
     sides = [pass_on(tokens, strip(0), right), pass_on(tokens, strip(0), left)]
 
     def make(src, which, owner, target):
@@ -326,44 +330,41 @@
     arrived(to_z[1])
     to_z[2] = swap(2)
     spread(1)
-    over = [
-        pass_on(tokens.at[pl.ds(0, half)], halfway.at[0], up),
-        pass_on(tokens.at[pl.ds(half, half)], halfway.at[1], down),
-    ]
     for copy in enter:
         copy.wait()
     for copy in leave:
         copy.start()
     ends = tokens_far(sides, False)
-    relay(0)
     arrived(over)
     over = [
         pass_on(halfway.at[0], origin(-2, 0), up),
         pass_on(halfway.at[1], origin(2, 1), down),
     ]
+    relay(0)
+    arrived(over)
+    sides = [pass_on(strip(0, True), strip(0, True), to) for to in (right, left)]
     arrived(to_z[2])
     to_z[3] = swap(3)
     spread(2)
     relay(1)
+    ends += tokens_far(sides, True)
     finish(0)
-    arrived(over)
-    sides = [pass_on(strip(0, True), strip(0, True), to) for to in (right, left)]
-    arrived(to_z[3])
-    spread(3)
-    ends += tokens_far(sides, True)
-    relay(2)
-    finish(1)
     arrived(ends)
     for copy in stay:
         copy.wait()
-    normalize(0, rows)
-    relay(3)
-    finish(2)
+    normalize(0, rows // 2)
+    arrived(to_z[3])
+    spread(3)
+    relay(2)
+    normalize(rows // 2, rows)
+    finish(1)
     project(
         modulated, w_in, hidden, 256, functools.partial(jax.nn.gelu, approximate=True)
     )
+    relay(3)
+    finish(2)
+    project(hidden, w_out, part, 512, lambda tile: tile)
     finish(3)
-    project(hidden, w_out, part, 512, lambda tile: tile)
     for copy in leave:
         copy.wait()
     for copy in to_core:

time: 157 us -> 162 us (1.032)
  the two profiles are of different devices: /device:TPU:40 before, /device:TPU:48 now
where the time goes in v7:
time: 162 us; the launch traced here: 163 us
  Pallas kernels  156 us (96%)
  matrix products  3.37 us (2%)
  other arithmetic  2.36 us (1%)
    pallas_call x1, Pallas kernels, gather_rows(): pl.pallas_call(gather_kernel, out_shape=(jax.ShapeDtypeStruct((rows, toke...  87.9 us
    pallas_call x1, Pallas kernels, reduce_rows(): pl.pallas_call(reduce_kernel, out_shape=jax.ShapeDtypeStruct((rows, width...  45.3 us
    pallas_call x1, Pallas kernels, attention(): pl.pallas_call(attend_kernel, out_shape=jax.ShapeDtypeStruct((rows, width...  23.2 us
    dot_general x1, matrix products, per_device(): jnp.dot(attended, w_attn_out, preferred_element_type=jnp.float32) + mlp_part  3.37 us

profile of v7, /device:TPU:48, one launch (start us, length us, event | category | flops | bytes accessed | tf_op | source)
XLA Modules:
  0.0 163.1 jit_solution(16839908387406047227)
XLA Ops:
  0.0 0.0 copy-start
  0.0 1.1 convert_reduce_fusion.ends_ref
  1.1 0.0 copy-start.3
  1.1 1.2 pad_add_fusion.table
  2.4 0.0 copy-done.3
  2.4 87.9 %gather_all.1 = (bf16[384,3072]{1,0:T(8,128)(2,1)}, bf16[12288,256]{1,0:T(8,128)(2,1)}, bf16[12288,256]{1,0:T(8,128)(2,1)}, f32[384,3072]{1,0:T(8,128)}) custom-call(s32[4]{0:T(128)} %copy-done.3, f32[3,4,3072]{2,1,0:T(4,128)} %modulation.3, bf16[384,384]{1,0:T(8,128)(2,1)} %tokens.1, bf16[384,256]{1,0:T(8,128)(2,1)} %keys.1, bf16[384,256]{1,0:T(8,128)(2,1)} %values.1, ...), custom_call_target="tpu_custom_call" | custom-call | tf_op jit(solution)/shard_map/gather_all/pallas_call | solution.py:381
  90.3 23.2 %attend.1 = bf16[384,256]{1,0:T(8,128)(2,1)} custom-call(s32[8]{0:T(128)} %pad_add_fusion.table, bf16[384,256]{1,0:T(8,128)(2,1)} %q_ref.1, bf16[12288,256]{1,0:T(8,128)(2,1)} %get-tuple-element.10.k_ref, bf16[12288,256]{1,0:T(8,128)(2,1)} %get-tuple-element.11.v_ref), custom_call_target="tpu_custom_call" | custom-call | flops 9663676416 | bytes 12582912 | tf_op jit(solution)/shard_map/attend/pallas_call | solution.py:117
  113.6 0.0 copy-done
  113.6 0.0 copy-start.1
  113.6 0.0 copy-start.2
  113.6 0.0 copy-start.4
  113.6 3.4 %add_convert_fusion.part = bf16[384,3072]{1,0:T(8,128)(2,1)S(1)} fusion(f32[384,3072]{1,0:T(8,128)} %get-tuple-element.12, bf16[384,256]{1,0:T(8,128)(2,1)} %attend.1, bf16[256,3072]{1,0:T(8,128)(2,1)S(1)} %copy-done), kind=kOutput, calls=%fused_computation | convolution fusion | flops 606339072 | bytes 8847360 | tf_op jit(solution)/shard_map/dot_general | solution.py:538
  117.0 0.0 copy-done.1
  117.0 0.0 copy-done.2
  117.0 0.0 copy-done.4
  117.0 45.3 %reduce_branch.1 = f32[48,3072]{1,0:T(8,128)S(1)} custom-call(s32[4]{0:T(128)S(1)} %copy-done.4, f32[3,4,3072]{2,1,0:T(4,128)S(1)} %copy-done.2, bf16[384,3072]{1,0:T(8,128)(2,1)S(1)} %copy-done.1, bf16[384,3072]{1,0:T(8,128)(2,1)S(1)} %add_convert_fusion.part), custom_call_target="tpu_custom_call" | custom-call | bytes 100000000 | tf_op jit(solution)/shard_map/reduce_branch/pallas_call | solution.py:499
  162.3 0.8 copy.12
Async XLA Ops:
  0.0 113.6 %copy-start = (bf16[256,3072]{1,0:T(8,128)(2,1)S(1)}, bf16[256,3072]{1,0:T(8,128)(2,1)}, u32[]{:S(2)}) copy-start(bf16[256,3072]{1,0:T(8,128)(2,1)} %param.18) | copy-start | bytes 4718596
  1.1 1.2 copy-start.3
  113.6 3.4 %copy-start.1 = (bf16[384,3072]{1,0:T(8,128)(2,1)S(1)}, bf16[384,3072]{1,0:T(8,128)(2,1)}, u32[]{:S(2)}) copy-start(bf16[384,3072]{1,0:T(8,128)(2,1)} %get-tuple-element.9.whole) | copy-start | bytes 7077892
  113.6 3.4 %copy-start.2 = (f32[3,4,3072]{2,1,0:T(4,128)S(1)}, f32[3,4,3072]{2,1,0:T(4,128)}, u32[]{:S(2)}) copy-start(f32[3,4,3072]{2,1,0:T(4,128)} %modulation.3) | copy-start | bytes 442372
  113.6 3.4 %copy-start.4 = (s32[4]{0:T(128)S(1)}, s32[4]{0:T(128)}, u32[]{:S(2)}) copy-start(s32[4]{0:T(128)} %copy-done.3) | copy-start | bytes 52
